TPU v7x, 32 devices: a whole 2x2x4 slice. The times are simulated.
32 devices in a mesh: dp: 8 (over z, y), tensor: 4 (over x, core).
Axes of the slice: x: 2, y: 2, z: 4, core: 2. Of those that a mesh axis runs over, the one named last changes fastest.
Arguments:
- layer_in: bfloat16 [16384, 768], P(('dp', 'tensor')), may hold values from -6 to 6
- ln1_gain: bfloat16 [768], P('dp'), may hold values from 0.5 to 1.5
- ln1_bias: bfloat16 [768], P('dp'), may hold values from -1.75 to 1.75
- query_weight: bfloat16 [768, 768], P('dp', 'tensor'), may hold values from -0.4375 to 0.4375
- query_bias: bfloat16 [768], P(('tensor', 'dp')), may hold values from -1.75 to 1.75
- key_weight: bfloat16 [768, 768], P('dp', 'tensor'), may hold values from -0.21875 to 0.21875
- value_weight: bfloat16 [768, 768], P('dp', 'tensor'), may hold values from -0.21875 to 0.21875
- value_bias: bfloat16 [768], P(('tensor', 'dp')), may hold values from -1.75 to 1.75
- inner_gain: bfloat16 [768], P(('tensor', 'dp')), may hold values from 0.5 to 1.5
- inner_bias: bfloat16 [768], P(('tensor', 'dp')), may hold values from -1.75 to 1.75
- output_weight: bfloat16 [768, 768], P('tensor', 'dp'), may hold values from -0.21875 to 0.21875
- output_bias: bfloat16 [768], P('dp'), may hold values from -1.75 to 1.75
- ln2_gain: bfloat16 [768], P('dp'), may hold values from 0.5 to 1.5
- ln2_bias: bfloat16 [768], P('dp'), may hold values from -1.75 to 1.75
- up_weight: bfloat16 [768, 3072], P('dp', 'tensor'), may hold values from -0.21875 to 0.21875
- up_bias: bfloat16 [3072], P(('tensor', 'dp')), may hold values from -1.75 to 1.75
- outer_gain: bfloat16 [3072], P(('tensor', 'dp')), may hold values from 0.5 to 1.5
- outer_bias: bfloat16 [3072], P(('tensor', 'dp')), may hold values from -1.75 to 1.75
- down_weight: bfloat16 [3072, 768], P('tensor', 'dp'), may hold values from -0.109375 to 0.109375
- down_bias: bfloat16 [768], P('dp'), may hold values from -1.75 to 1.75
- out_grad: bfloat16 [16384, 768], P(('dp', 'tensor')), may hold values from -12 to 12
- prefix: int32 [4], replicated, may hold values from 2560 to 3584, as said below
Outputs:
- layer_out: bfloat16 [16384, 768], P(('dp', 'tensor'))
- input_grad: float32 [16384, 768], P(('dp', 'tensor'))
- grad_ln1_gain: float32 [768], P('dp')
- grad_ln1_bias: float32 [768], P('dp')
- grad_query_weight: float32 [768, 768], P('dp', 'tensor')
- grad_query_bias: float32 [768], P(('tensor', 'dp'))
- grad_key_weight: float32 [768, 768], P('dp', 'tensor')
- grad_value_weight: float32 [768, 768], P('dp', 'tensor')
- grad_value_bias: float32 [768], P(('tensor', 'dp'))
- grad_inner_gain: float32 [768], P(('tensor', 'dp'))
- grad_inner_bias: float32 [768], P(('tensor', 'dp'))
- grad_output_weight: float32 [768, 768], P('tensor', 'dp')
- grad_output_bias: float32 [768], P('dp')
- grad_ln2_gain: float32 [768], P('dp')
- grad_ln2_bias: float32 [768], P('dp')
- grad_up_weight: float32 [768, 3072], P('dp', 'tensor')
- grad_up_bias: float32 [3072], P(('tensor', 'dp'))
- grad_outer_gain: float32 [3072], P(('tensor', 'dp'))
- grad_outer_bias: float32 [3072], P(('tensor', 'dp'))
- grad_down_weight: float32 [3072, 768], P('tensor', 'dp')
- grad_down_bias: float32 [768], P('dp')
Inputs may be any that keep to these rules, and one draw needn't show every extreme that they name: prefix[s] is the number of leading positions of sequence s that attend both ways; it reaches past the first 2048 positions in every sequence, and some sequence has exactly 3584.
All inputs are finite; a program needn't handle non-finite values.
Results may differ from a plain program's by a relative error of at most 0.017.
Values may be sent and summed in bfloat16 or wider, within the bound.
No kernel may reach another device: no remote copies, remote signals or barrier semaphores. Data moves between devices by JAX's collectives and lax.ppermute only.
A program may use at most 192 MiB of HBM per device.

v0:
```python
from functools import partial

import jax
import jax.numpy as jnp
from jax import lax
from jax.sharding import PartitionSpec as P

H = 12
DH = 64
FF = 3072
SEG1 = 2048


epsilon = 1e-05
masked_score = -1000000000.0
score_scale = 0.125


def from_partner(value, axis, stride):
    mask = 2**stride
    pairs = [(source, source ^ mask) for source in range(lax.axis_size(axis))]
    return lax.ppermute(value, axis, pairs)


def contract(left_side, right_side, left_dim, right_dim):
    return lax.dot_general(
        left_side,
        right_side,
        (((left_dim,), (right_dim,)), ((), ())),
        preferred_element_type=jnp.float32,
    )


def gather_rows(values):
    return lax.all_gather(values, "tensor", axis=0, tiled=True)


def scatter_rows(values):
    return lax.psum_scatter(values, "tensor", scatter_dimension=0, tiled=True)


def cross_sums(first_part, second_part):
    return lax.psum((first_part, second_part), "tensor")


def fetch_first(
    query_weight,
    key_weight,
    value_weight,
    output_flip,
    up_weight,
    down_flip,
    query_bias,
    value_bias,
    inner_gain,
    inner_bias,
    up_bias,
    outer_gain,
    outer_bias,
    ln1_gain,
    ln1_bias,
    output_bias,
    ln2_gain,
    ln2_bias,
    down_bias,
):
    return (
        lax.all_gather(query_weight, "dp", axis=0, tiled=True),
        lax.all_gather(key_weight, "dp", axis=0, tiled=True),
        lax.all_gather(value_weight, "dp", axis=0, tiled=True),
        lax.all_gather(output_flip, "dp", axis=0, tiled=True),
        lax.all_gather(up_weight, "dp", axis=0, tiled=True),
        lax.all_gather(down_flip, "dp", axis=0, tiled=True),
        lax.all_gather(query_bias, "dp", axis=0, tiled=True),
        lax.all_gather(value_bias, "dp", axis=0, tiled=True),
        lax.all_gather(inner_gain, "dp", axis=0, tiled=True),
        lax.all_gather(inner_bias, "dp", axis=0, tiled=True),
        lax.all_gather(up_bias, "dp", axis=0, tiled=True),
        lax.all_gather(outer_gain, "dp", axis=0, tiled=True),
        lax.all_gather(outer_bias, "dp", axis=0, tiled=True),
        lax.all_gather(ln1_gain, "dp", axis=0, tiled=True),
        lax.all_gather(ln1_bias, "dp", axis=0, tiled=True),
        lax.all_gather(output_bias, "dp", axis=0, tiled=True),
        lax.all_gather(ln2_gain, "dp", axis=0, tiled=True),
        lax.all_gather(ln2_bias, "dp", axis=0, tiled=True),
        lax.all_gather(down_bias, "dp", axis=0, tiled=True),
    )


def fetch_again(query_weight, key_weight, value_weight, output_flip, up_weight, down_flip):
    return (
        lax.all_gather(query_weight, "dp", axis=0, tiled=True),
        lax.all_gather(key_weight, "dp", axis=0, tiled=True),
        lax.all_gather(value_weight, "dp", axis=0, tiled=True),
        lax.all_gather(output_flip, "dp", axis=0, tiled=True),
        lax.all_gather(up_weight, "dp", axis=0, tiled=True),
        lax.all_gather(down_flip, "dp", axis=0, tiled=True),
    )


def norm_local(values, norm_gain, norm_shift):
    middle_point = jnp.mean(values, axis=1, keepdims=True)
    spread = jnp.mean(values * values, axis=1, keepdims=True) - middle_point * middle_point
    scaling = lax.rsqrt(spread + epsilon)
    normed = (values - middle_point) * scaling
    return (normed * norm_gain + norm_shift, normed, scaling)


def norm_local_back(grad_out, normed, scaling, norm_gain):
    grad_hat = grad_out * norm_gain
    return scaling * (
        grad_hat
        - jnp.mean(grad_hat, axis=1, keepdims=True)
        - normed * jnp.mean(grad_hat * normed, axis=1, keepdims=True)
    )


def norm_split(values, norm_gain, norm_shift, full_width):
    summed, squares = cross_sums(jnp.sum(values, axis=1), jnp.sum(values * values, axis=1))
    middle_point = (summed / full_width)[:, None]
    spread = (squares / full_width)[:, None] - middle_point * middle_point
    scaling = lax.rsqrt(spread + epsilon)
    normed = (values - middle_point) * scaling
    return (normed * norm_gain + norm_shift, normed, scaling)


def norm_split_back(grad_out, normed, scaling, norm_gain, full_width):
    grad_hat = grad_out * norm_gain
    summed, paired = cross_sums(jnp.sum(grad_hat, axis=1), jnp.sum(grad_hat * normed, axis=1))
    return scaling * (
        grad_hat - (summed / full_width)[:, None] - normed * (paired / full_width)[:, None]
    )


def allowed_pairs(query_pos, key_pos, prefix_len):
    return (key_pos[None, :] <= query_pos[:, None]) | (key_pos[None, :] < prefix_len)


def masked_scores(block_query, key_rows, block_pos, key_pos, prefix_len):
    scores = contract(block_query, key_rows, 1, 1) * score_scale
    return jnp.where(allowed_pairs(block_pos, key_pos, prefix_len), scores, masked_score)


def attend_forward(query_rows, key_rows, value_rows, query_pos, key_pos, prefix_len):
    row_count = query_rows.shape[0]
    stride_rows = min(512, row_count)

    def one_block(shift_amount):
        block_query = lax.dynamic_slice_in_dim(query_rows, shift_amount, stride_rows)
        block_pos = lax.dynamic_slice_in_dim(query_pos, shift_amount, stride_rows)
        scores = masked_scores(block_query, key_rows, block_pos, key_pos, prefix_len)
        row_top = jnp.max(scores, axis=1, keepdims=True)
        log_total = row_top[:, 0] + jnp.log(jnp.sum(jnp.exp(scores - row_top), axis=1))
        attention_weights = jnp.exp(scores - log_total[:, None]).astype(jnp.bfloat16)
        return (
            jnp.dot(attention_weights, value_rows, preferred_element_type=jnp.float32),
            log_total,
        )

    offsets = jnp.arange(row_count // stride_rows, dtype=jnp.int32) * stride_rows
    outputs, logs = lax.map(one_block, offsets)
    return (outputs.reshape(row_count, -1), logs.reshape(row_count))


def attend_backward(
    query_rows,
    key_rows,
    value_rows,
    query_pos,
    key_pos,
    prefix_len,
    log_total,
    grad_out,
    logsum_gradient,
):
    row_count = query_rows.shape[0]
    stride_rows = min(512, row_count)

    def one_block(running, shift_amount):
        key_grad, value_grad = running
        block_query = lax.dynamic_slice_in_dim(query_rows, shift_amount, stride_rows)
        block_pos = lax.dynamic_slice_in_dim(query_pos, shift_amount, stride_rows)
        block_log = lax.dynamic_slice_in_dim(log_total, shift_amount, stride_rows)
        block_grad = lax.dynamic_slice_in_dim(grad_out, shift_amount, stride_rows)
        block_log_gradient = lax.dynamic_slice_in_dim(logsum_gradient, shift_amount, stride_rows)
        scores = masked_scores(block_query, key_rows, block_pos, key_pos, prefix_len)
        attention_weights = jnp.exp(scores - block_log[:, None])
        weight_gradient = contract(block_grad, value_rows, 1, 1)
        middle_point = jnp.sum(attention_weights * weight_gradient, axis=1, keepdims=True)
        score_gradient = (
            attention_weights * (weight_gradient - middle_point + block_log_gradient[:, None])
        ).astype(jnp.bfloat16)
        query_grad = (
            jnp.dot(score_gradient, key_rows, preferred_element_type=jnp.float32) * score_scale
        )
        key_grad = key_grad + contract(score_gradient, block_query, 0, 0) * score_scale
        value_grad = value_grad + contract(attention_weights.astype(jnp.bfloat16), block_grad, 0, 0)
        return ((key_grad, value_grad), query_grad)

    offsets = jnp.arange(row_count // stride_rows, dtype=jnp.int32) * stride_rows
    zero_keys = jnp.zeros(key_rows.shape, jnp.float32)
    (key_grad, value_grad), query_grads = lax.scan(one_block, (zero_keys, zero_keys), offsets)
    return (query_grads.reshape(row_count, -1), key_grad, value_grad)


def merge_forward(near_out, near_log, far_out, far_log, parity):
    half_rows = near_out.shape[0] // 2
    near_pairs = near_out.reshape(half_rows, 2, -1)
    near_logs = near_log.reshape(half_rows, 2)
    slot_pick = jnp.arange(2, dtype=jnp.int32)[None, :] == parity
    row_top = jnp.where(slot_pick, jnp.maximum(near_logs, far_log[:, None]), near_logs)
    near_weight = jnp.exp(near_logs - row_top)
    far_weight = jnp.where(
        slot_pick, jnp.exp(jnp.where(slot_pick, far_log[:, None] - row_top, 0.0)), 0.0
    )
    row_total = near_weight + far_weight
    near_share = near_weight / row_total
    far_share = far_weight / row_total
    merged = near_share[:, :, None] * near_pairs + far_share[:, :, None] * far_out[:, None, :]
    return (merged, near_share, far_share)


def dilate(row_block, parity):
    paired = row_block.reshape(row_block.shape[0] // 2, 2, row_block.shape[1], row_block.shape[2])
    return jnp.where((parity == 1)[None, :, None], paired[:, 1], paired[:, 0])


def undilate(row_block, parity):
    slot_pick = (jnp.arange(2, dtype=jnp.int32)[:, None] == parity[None, :])[None, :, :, None]
    spread_rows = jnp.where(slot_pick, row_block[:, None], 0.0)
    return spread_rows.reshape(row_block.shape[0] * 2, row_block.shape[1], row_block.shape[2])


def local(
    layer_in,
    ln1_gain,
    ln1_bias,
    query_weight,
    query_bias,
    key_weight,
    value_weight,
    value_bias,
    inner_gain,
    inner_bias,
    output_weight,
    output_bias,
    ln2_gain,
    ln2_bias,
    up_weight,
    up_bias,
    outer_gain,
    outer_bias,
    down_weight,
    down_bias,
    out_grad,
    prefix,
):
    heads_local = H // lax.axis_size("tensor")
    local_width = heads_local * DH
    half_rows = SEG1 // 2
    device_pos = lax.axis_index("dp")
    odd_half = device_pos % 2 == 1
    base_pos = device_pos % 2 * SEG1
    prefix_len = lax.dynamic_index_in_dim(prefix, device_pos // 2, keepdims=False)
    parity = (lax.axis_index("tensor") * heads_local + jnp.arange(heads_local, dtype=jnp.int32)) % 2
    near_pos = base_pos + jnp.arange(SEG1, dtype=jnp.int32)
    far_key_base = 2 * jnp.arange(SEG1, dtype=jnp.int32)
    far_query_base = base_pos + 2 * jnp.arange(half_rows, dtype=jnp.int32)
    fetched = fetch_first(
        query_weight,
        key_weight,
        value_weight,
        output_weight.T,
        up_weight,
        down_weight.T,
        query_bias,
        value_bias,
        inner_gain,
        inner_bias,
        up_bias,
        outer_gain,
        outer_bias,
        ln1_gain,
        ln1_bias,
        output_bias,
        ln2_gain,
        ln2_bias,
        down_bias,
    )
    full_query, full_key, full_value, full_output, full_up, full_down = fetched[:6]
    vectors = [piece.astype(jnp.float32) for piece in fetched[6:]]
    (
        query_shift,
        value_shift,
        inner_scale,
        inner_shift,
        up_shift,
        outer_scale,
        outer_shift,
        norm1_scale,
        norm1_shift,
        output_shift,
        norm2_scale,
        norm2_shift,
        down_shift,
    ) = vectors
    layer_float = layer_in.astype(jnp.float32)
    normed_one, hat_one, scale_one = norm_local(layer_float, norm1_scale, norm1_shift)
    hidden_one = gather_rows(normed_one.astype(jnp.bfloat16))
    query_rows = (
        (jnp.dot(hidden_one, full_query, preferred_element_type=jnp.float32) + query_shift)
        .astype(jnp.bfloat16)
        .reshape(SEG1, heads_local, DH)
    )
    key_rows = (
        jnp.dot(hidden_one, full_key, preferred_element_type=jnp.float32)
        .astype(jnp.bfloat16)
        .reshape(SEG1, heads_local, DH)
    )
    value_rows = (
        (jnp.dot(hidden_one, full_value, preferred_element_type=jnp.float32) + value_shift)
        .astype(jnp.bfloat16)
        .reshape(SEG1, heads_local, DH)
    )
    far_query = dilate(query_rows, parity)
    far_key_own = dilate(key_rows, parity)
    far_value_own = dilate(value_rows, parity)
    packed = jnp.concatenate(
        (key_rows.reshape(SEG1, local_width), value_rows.reshape(SEG1, local_width)), axis=1
    )
    arrived = from_partner(packed, "dp", 0)
    far_key_peer = dilate(arrived[:, :local_width].reshape(SEG1, heads_local, DH), parity)
    far_value_peer = dilate(arrived[:, local_width:].reshape(SEG1, heads_local, DH), parity)
    far_key_all = jnp.concatenate(
        (
            jnp.where(odd_half, far_key_peer, far_key_own),
            jnp.where(odd_half, far_key_own, far_key_peer),
        ),
        axis=0,
    )
    far_value_all = jnp.concatenate(
        (
            jnp.where(odd_half, far_value_peer, far_value_own),
            jnp.where(odd_half, far_value_own, far_value_peer),
        ),
        axis=0,
    )
    stored = []
    merged_heads = []
    for head_index in range(heads_local):
        near_out, near_log = attend_forward(
            query_rows[:, head_index],
            key_rows[:, head_index],
            value_rows[:, head_index],
            near_pos,
            near_pos,
            prefix_len,
        )
        far_out, far_log = attend_forward(
            far_query[:, head_index],
            far_key_all[:, head_index],
            far_value_all[:, head_index],
            far_query_base + parity[head_index],
            far_key_base + parity[head_index],
            prefix_len,
        )
        merged, near_share, far_share = merge_forward(
            near_out, near_log, far_out, far_log, parity[head_index]
        )
        stored.append((near_out, near_log, far_out, far_log, merged, near_share, far_share))
        merged_heads.append(merged.reshape(SEG1, DH))
    attended = jnp.stack(merged_heads, axis=1).reshape(SEG1, local_width)
    inner_normed, inner_hat, inner_scaling = norm_split(attended, inner_scale, inner_shift, H * DH)
    inner_rows = inner_normed.astype(jnp.bfloat16)
    projected = scatter_rows(contract(inner_rows, full_output, 1, 1))
    middle = layer_float + projected + output_shift
    normed_two, hat_two, scale_two = norm_local(middle, norm2_scale, norm2_shift)
    hidden_two = gather_rows(normed_two.astype(jnp.bfloat16))
    up_rows = jnp.dot(hidden_two, full_up, preferred_element_type=jnp.float32) + up_shift
    activated, gelu_back = jax.vjp(partial(jax.nn.gelu, approximate=False), up_rows)
    outer_normed, outer_hat, outer_scaling = norm_split(activated, outer_scale, outer_shift, FF)
    outer_rows = outer_normed.astype(jnp.bfloat16)
    layer_out = middle + scatter_rows(contract(outer_rows, full_down, 1, 1)) + down_shift
    refetched = fetch_again(
        query_weight, key_weight, value_weight, output_weight.T, up_weight, down_weight.T
    )
    back_query, back_key, back_value, back_output, back_up, back_down = refetched
    grad_float = out_grad.astype(jnp.float32)
    grad_rows = gather_rows(out_grad)
    grad_down_shift = jnp.sum(grad_float, axis=0)
    grad_down_flip = contract(grad_rows, outer_rows, 0, 0)
    outer_grad = jnp.dot(grad_rows, back_down, preferred_element_type=jnp.float32)
    grad_outer_scale = jnp.sum(outer_grad * outer_hat, axis=0)
    grad_outer_shift = jnp.sum(outer_grad, axis=0)
    activated_grad = norm_split_back(outer_grad, outer_hat, outer_scaling, outer_scale, FF)
    up_grad = gelu_back(activated_grad)[0].astype(jnp.bfloat16)
    grad_up_shift = jnp.sum(up_grad.astype(jnp.float32), axis=0)
    grad_up_w = contract(hidden_two, up_grad, 0, 0)
    hidden_two_grad = scatter_rows(contract(up_grad, back_up, 1, 1))
    grad_norm2_scale = jnp.sum(hidden_two_grad * hat_two, axis=0)
    grad_norm2_shift = jnp.sum(hidden_two_grad, axis=0)
    middle_grad = grad_float + norm_local_back(hidden_two_grad, hat_two, scale_two, norm2_scale)
    middle_low = middle_grad.astype(jnp.bfloat16)
    grad_output_shift = jnp.sum(middle_low.astype(jnp.float32), axis=0)
    middle_rows = gather_rows(middle_low)
    grad_output_flip = contract(middle_rows, inner_rows, 0, 0)
    inner_grad = jnp.dot(middle_rows, back_output, preferred_element_type=jnp.float32)
    grad_inner_scale = jnp.sum(inner_grad * inner_hat, axis=0)
    grad_inner_shift = jnp.sum(inner_grad, axis=0)
    attended_grad = norm_split_back(inner_grad, inner_hat, inner_scaling, inner_scale, H * DH)
    grad_heads = attended_grad.reshape(SEG1, heads_local, DH)
    near_query_list, near_key_list, near_value_list = ([], [], [])
    far_query_list, far_key_list, far_value_list = ([], [], [])
    for head_index in range(heads_local):
        near_out, near_log, far_out, far_log, merged, near_share, far_share = stored[head_index]
        grad_merged = grad_heads[:, head_index].reshape(half_rows, 2, DH)
        near_pairs = near_out.reshape(half_rows, 2, DH)
        near_grad = (near_share[:, :, None] * grad_merged).reshape(SEG1, DH)
        far_grad = jnp.sum(far_share[:, :, None] * grad_merged, axis=1)
        near_log_grad = (near_share * jnp.sum(grad_merged * (near_pairs - merged), axis=2)).reshape(
            SEG1
        )
        far_log_grad = jnp.sum(
            far_share * jnp.sum(grad_merged * (far_out[:, None, :] - merged), axis=2), axis=1
        )
        near_q, near_k, near_v = attend_backward(
            query_rows[:, head_index],
            key_rows[:, head_index],
            value_rows[:, head_index],
            near_pos,
            near_pos,
            prefix_len,
            near_log,
            near_grad.astype(jnp.bfloat16),
            near_log_grad,
        )
        far_q, far_k, far_v = attend_backward(
            far_query[:, head_index],
            far_key_all[:, head_index],
            far_value_all[:, head_index],
            far_query_base + parity[head_index],
            far_key_base + parity[head_index],
            prefix_len,
            far_log,
            far_grad.astype(jnp.bfloat16),
            far_log_grad,
        )
        near_query_list.append(near_q)
        near_key_list.append(near_k)
        near_value_list.append(near_v)
        far_query_list.append(far_q)
        far_key_list.append(far_k)
        far_value_list.append(far_v)
    far_key_grad = jnp.stack(far_key_list, axis=1)
    far_value_grad = jnp.stack(far_value_list, axis=1)
    own_key = jnp.where(odd_half, far_key_grad[half_rows:], far_key_grad[:half_rows])
    peer_key = jnp.where(odd_half, far_key_grad[:half_rows], far_key_grad[half_rows:])
    own_value = jnp.where(odd_half, far_value_grad[half_rows:], far_value_grad[:half_rows])
    peer_value = jnp.where(odd_half, far_value_grad[:half_rows], far_value_grad[half_rows:])
    whole_grads = jnp.concatenate(
        (
            undilate(peer_key, parity).reshape(SEG1, local_width),
            undilate(peer_value, parity).reshape(SEG1, local_width),
        ),
        axis=1,
    )
    returned = from_partner(whole_grads.astype(jnp.bfloat16), "dp", 0).astype(whole_grads.dtype)
    back_key_rows = dilate(returned[:, :local_width].reshape(SEG1, heads_local, DH), parity)
    back_value_rows = dilate(returned[:, local_width:].reshape(SEG1, heads_local, DH), parity)
    query_total = jnp.stack(near_query_list, axis=1) + undilate(
        jnp.stack(far_query_list, axis=1), parity
    )
    key_total = jnp.stack(near_key_list, axis=1) + undilate(own_key + back_key_rows, parity)
    value_total = jnp.stack(near_value_list, axis=1) + undilate(own_value + back_value_rows, parity)
    query_low = query_total.reshape(SEG1, local_width).astype(jnp.bfloat16)
    key_low = key_total.reshape(SEG1, local_width).astype(jnp.bfloat16)
    value_low = value_total.reshape(SEG1, local_width).astype(jnp.bfloat16)
    grad_query_shift = jnp.sum(query_low.astype(jnp.float32), axis=0)
    grad_value_shift = jnp.sum(value_low.astype(jnp.float32), axis=0)
    grad_query_w = contract(hidden_one, query_low, 0, 0)
    grad_key_w = contract(hidden_one, key_low, 0, 0)
    grad_value_w = contract(hidden_one, value_low, 0, 0)
    hidden_one_grad = scatter_rows(
        contract(query_low, back_query, 1, 1)
        + contract(key_low, back_key, 1, 1)
        + contract(value_low, back_value, 1, 1)
    )
    grad_norm1_scale = jnp.sum(hidden_one_grad * hat_one, axis=0)
    grad_norm1_shift = jnp.sum(hidden_one_grad, axis=0)
    input_grad = middle_grad + norm_local_back(hidden_one_grad, hat_one, scale_one, norm1_scale)
    (
        summed_norm1_scale,
        summed_norm1_shift,
        summed_output_shift,
        summed_norm2_scale,
        summed_norm2_shift,
        summed_down_shift,
    ) = lax.psum(
        (
            grad_norm1_scale,
            grad_norm1_shift,
            grad_output_shift,
            grad_norm2_scale,
            grad_norm2_shift,
            grad_down_shift,
        ),
        "tensor",
    )
    reduced = (
        lax.psum_scatter(grad_query_w, "dp", scatter_dimension=0, tiled=True),
        lax.psum_scatter(grad_key_w, "dp", scatter_dimension=0, tiled=True),
        lax.psum_scatter(grad_value_w, "dp", scatter_dimension=0, tiled=True),
        lax.psum_scatter(grad_output_flip, "dp", scatter_dimension=0, tiled=True),
        lax.psum_scatter(grad_up_w, "dp", scatter_dimension=0, tiled=True),
        lax.psum_scatter(grad_down_flip, "dp", scatter_dimension=0, tiled=True),
        lax.psum_scatter(grad_query_shift, "dp", scatter_dimension=0, tiled=True),
        lax.psum_scatter(grad_value_shift, "dp", scatter_dimension=0, tiled=True),
        lax.psum_scatter(grad_inner_scale, "dp", scatter_dimension=0, tiled=True),
        lax.psum_scatter(grad_inner_shift, "dp", scatter_dimension=0, tiled=True),
        lax.psum_scatter(grad_up_shift, "dp", scatter_dimension=0, tiled=True),
        lax.psum_scatter(grad_outer_scale, "dp", scatter_dimension=0, tiled=True),
        lax.psum_scatter(grad_outer_shift, "dp", scatter_dimension=0, tiled=True),
        lax.psum_scatter(summed_norm1_scale, "dp", scatter_dimension=0, tiled=True),
        lax.psum_scatter(summed_norm1_shift, "dp", scatter_dimension=0, tiled=True),
        lax.psum_scatter(summed_output_shift, "dp", scatter_dimension=0, tiled=True),
        lax.psum_scatter(summed_norm2_scale, "dp", scatter_dimension=0, tiled=True),
        lax.psum_scatter(summed_norm2_shift, "dp", scatter_dimension=0, tiled=True),
        lax.psum_scatter(summed_down_shift, "dp", scatter_dimension=0, tiled=True),
    )
    return (
        layer_out.astype(jnp.bfloat16),
        input_grad,
        reduced[13],
        reduced[14],
        reduced[0],
        reduced[6],
        reduced[1],
        reduced[2],
        reduced[7],
        reduced[8],
        reduced[9],
        reduced[3].T,
        reduced[15],
        reduced[16],
        reduced[17],
        reduced[4],
        reduced[10],
        reduced[11],
        reduced[12],
        reduced[5].T,
        reduced[18],
    )


def solution(mesh):
    in_specs = (
        P(("dp", "tensor"), None),
        P("dp"),
        P("dp"),
        P("dp", "tensor"),
        P(("tensor", "dp")),
        P("dp", "tensor"),
        P("dp", "tensor"),
        P(("tensor", "dp")),
        P(("tensor", "dp")),
        P(("tensor", "dp")),
        P("tensor", "dp"),
        P("dp"),
        P("dp"),
        P("dp"),
        P("dp", "tensor"),
        P(("tensor", "dp")),
        P(("tensor", "dp")),
        P(("tensor", "dp")),
        P("tensor", "dp"),
        P("dp"),
        P(("dp", "tensor"), None),
        P(),
    )
    out_specs = (
        P(("dp", "tensor"), None),
        P(("dp", "tensor"), None),
        P("dp"),
        P("dp"),
        P("dp", "tensor"),
        P(("tensor", "dp")),
        P("dp", "tensor"),
        P("dp", "tensor"),
        P(("tensor", "dp")),
        P(("tensor", "dp")),
        P(("tensor", "dp")),
        P("tensor", "dp"),
        P("dp"),
        P("dp"),
        P("dp"),
        P("dp", "tensor"),
        P(("tensor", "dp")),
        P(("tensor", "dp")),
        P(("tensor", "dp")),
        P("tensor", "dp"),
        P("dp"),
    )
    return jax.shard_map(local, mesh=mesh, in_specs=in_specs, out_specs=out_specs, check_vma=False)
```

profile of v0, /device:TPU:0, one launch (start us, length us, event | category | flops | bytes accessed | tf_op | source)
XLA Modules:
  0.0 1782.6 jit_solution(434028498062962160)
XLA Ops:
  21.7 39.5 %all-reduce.32 = (bf16[768]{0:T(1024)(128)(2,1)S(1)}, bf16[768]{0:T(1024)(128)(2,1)S(1)}, bf16[192]{0:T(256)(128)(2,1)S(1)}, bf16[192]{0:T(256)(128)(2,1)S(1)}, ...) all-reduce(bf16[768]{0:T(1024)(128)(2,1)S(1)} %dynamic-update-slice, ...), channel_id=1, replica_groups=mesh['dp'=8,'tensor'=4] {'dp'}, use_global_device_ids=true, to_apply=%add.1 | all-reduce | flops 7680 | bytes 30720
  74.7 31.1 %all_gather.81 = bf16[768,192]{1,0:T(8,128)(2,1)S(1)} all-gather(bf16[96,192]{1,0:T(8,128)(2,1)S(1)} %copy-done.141), channel_id=1, replica_groups=mesh['dp'=8,'tensor'=4] {'dp'}, dimensions={0}, use_global_device_ids=true | all-gather | bytes 331776 | tf_op jit(solution)/shard_map/all_gather | solution.py:70
  105.7 31.0 %all_gather.80 = bf16[768,192]{1,0:T(8,128)(2,1)S(1)} all-gather(bf16[96,192]{1,0:T(8,128)(2,1)S(1)} %copy-done.142), channel_id=1, replica_groups=mesh['dp'=8,'tensor'=4] {'dp'}, dimensions={0}, use_global_device_ids=true | all-gather | bytes 331776 | tf_op jit(solution)/shard_map/all_gather | solution.py:69
  136.7 31.1 %all_gather.78 = bf16[768,192]{1,0:T(8,128)(2,1)S(1)} all-gather(bf16[96,192]{1,0:T(8,128)(2,1)S(1)} %copy-done.143), channel_id=1, replica_groups=mesh['dp'=8,'tensor'=4] {'dp'}, dimensions={0}, use_global_device_ids=true | all-gather | bytes 331776 | tf_op jit(solution)/shard_map/all_gather | solution.py:68
  167.8 33.4 %all_gather.85 = bf16[768,192]{1,0:T(8,128)(2,1)} all-gather(bf16[96,192]{1,0:T(8,128)(2,1)S(1)} %bitcast.631), channel_id=1, replica_groups=mesh['dp'=8,'tensor'=4] {'dp'}, dimensions={0}, use_global_device_ids=true | all-gather | bytes 331776 | tf_op jit(solution)/shard_map/all_gather | solution.py:71
  216.1 27.3 %while.165 = (s32[]{:T(128)}, f32[4,512,64]{1,2,0:T(8,128)}, f32[4,512]{1,0:T(4,128)S(1)}, s32[2048]{0:T(1024)S(1)}, s32[4]{0:T(128)S(1)}, /*index=5*/s32[]{:T(1...) while((s32[]{:T(128)}, f32[4,512,64]{1,2,0:T(8,128)}, ...), condition=%wide.region_5.6_spmd, body=%wide.region_2.5_spmd.sunk | while | flops 277874176 | bytes 13677235 | solution.py:161
  248.9 27.2 %while.166 = (s32[]{:T(128)}, f32[4,512,64]{1,2,0:T(8,128)}, f32[4,512]{1,0:T(4,128)S(1)}, s32[2048]{0:T(1024)S(1)}, s32[4]{0:T(128)S(1)}, /*index=5*/s32[]{:T(1...) while((s32[]{:T(128)}, f32[4,512,64]{1,2,0:T(8,128)}, ...), condition=%wide.region_13.14_spmd, body=%wide.region_10.13_spmd.sunk | while | flops 277874176 | bytes 13677235 | solution.py:161
  281.1 27.2 %while.167 = (s32[]{:T(128)}, f32[4,512,64]{1,2,0:T(8,128)}, f32[4,512]{1,0:T(4,128)S(1)}, s32[2048]{0:T(1024)S(1)}, s32[4]{0:T(128)S(1)}, /*index=5*/s32[]{:T(1...) while((s32[]{:T(128)}, f32[4,512,64]{1,2,0:T(8,128)}, ...), condition=%wide.region_21.22_spmd, body=%wide.region_18.21_spmd.sunk | while | flops 277874176 | bytes 13677235 | solution.py:161
  316.2 5.1 reshape_reshape.51
  332.9 4.9 broadcast_select_fusion.3
  352.2 4.6 fusion.269
  356.8 15.0 while.168
  377.1 16.8 while.169
  401.7 17.2 while.170
  433.1 10.1 all-reduce.31
  444.1 4.5 fusion.247
  452.1 54.6 %reduce-scatter.13.cloned.1.call-done = f32[512,768]{1,0:T(8,128)} async-done(((f32[2048,768]{1,0:T(8,128)}), f32[512,768]{1,0:T(8,128)}) %reduce-scatter.13.cloned.1.call-update) | async-done | bytes 1572880 | tf_op jit(solution)/shard_map/reduce_scatter | solution.py:39
  514.4 8.6 all-gather.15.cloned.1.call-done
  523.0 8.2 fusion.275
  531.1 6.8 copy.412
  537.9 28.6 %all-gather.11.cloned.1.call-done = bf16[768,768]{1,0:T(8,128)(2,1)} async-done(((bf16[96,768]{1,0:T(8,128)(2,1)}), bf16[768,768]{1,0:T(8,128)(2,1)}) %all-gather.11.cloned.1.call-update) | async-done | bytes 1179664 | tf_op jit(solution)/shard_map/all_gather | solution.py:72
  566.5 28.9 %all-gather.9.cloned.1.call-done = bf16[2048,768]{1,0:T(8,128)(2,1)} async-done(((bf16[512,768]{1,0:T(8,128)(2,1)}), bf16[2048,768]{1,0:T(8,128)(2,1)}) %all-gather.9.cloned.1.call-update) | async-done | bytes 3145744 | tf_op jit(solution)/shard_map/all_gather | solution.py:35
  595.4 22.2 %fusion.248 = (f32[2048]{0:T(1024)}, f32[2048]{0:T(1024)}, f32[2048,768]{0,1:T(8,128)}, f32[2048,768]{0,1:T(8,128)}, f32[2048,768]{0,1:T(8,128)}) fusion(f32[768]{0:T(1024)} %convert_element_type.200, bf16[2048,768]{1,0:T(8,128)(2,1)} %all-gather.9.cloned.1.call-done, bf16[768,768]{1,0:T(8,128)(2,1)} %all-gather.11.cloned.1.call-done), kind=kOutput, calls=%fused_computation.486 | convolution fusion | flops 2522869760 | bytes 23219200 | tf_op jit(solution)/shard_map/dot_general | solution.py:379
  617.5 11.4 all-reduce.30
  629.7 6.5 multiply_reduce_fusion.6
  636.2 11.3 all-reduce.29
  648.8 13.3 convert_reduce_fusion
  663.8 4.7 fusion.277
  668.8 8.1 fusion.276
  678.2 50.5 %reduce-scatter.17.cloned.1.call-done = f32[512,768]{1,0:T(8,128)} async-done(((f32[2048,768]{1,0:T(8,128)}), f32[512,768]{1,0:T(8,128)}) %reduce-scatter.17.cloned.1.call-update) | async-done | bytes 1572880 | tf_op jit(solution)/shard_map/reduce_scatter | solution.py:39
  732.5 57.4 %reduce-scatter.15.cloned.1.call-done = f32[512,768]{1,0:T(8,128)} async-done(((f32[2048,768]{1,0:T(8,128)}), f32[512,768]{1,0:T(8,128)}) %reduce-scatter.15.cloned.1.call-update) | async-done | bytes 1572880 | tf_op jit(solution)/shard_map/reduce_scatter | solution.py:39
  790.0 5.3 convert_reduce_fusion.3
  808.7 15.2 all-gather.17.cloned.1.call-done
  824.0 4.9 multiply_reduce_fusion.12
  828.9 11.3 all-reduce.28
  861.0 5.7 multiply_reduce_fusion.24
  867.5 39.2 %while.174 = (s32[]{:T(128)}, f32[2048,64]{0,1:T(8,128)}, f32[2048,64]{0,1:T(8,128)}, f32[2,512,64]{1,0,2:T(2,128)}, s32[2]{0:T(128)S(1)}, /*index=5*/s32[1024]{...) while((s32[]{:T(128)}, f32[2048,64]{0,1:T(8,128)}, ...), condition=%wide.region_68.69_spmd.clone, body=%wide.region_66.68_spmd.clone.sunk | while | flops 684369408 | bytes 53389692 | solution.py:202
  909.5 6.6 multiply_reduce_fusion.22
  916.9 42.0 %while.175 = (s32[]{:T(128)}, f32[2048,64]{0,1:T(8,128)}, f32[2048,64]{0,1:T(8,128)S(1)}, f32[2,512,64]{1,0,2:T(2,128)}, s32[2]{0:T(128)S(1)}, /*index=5*/s32[10...) while((s32[]{:T(128)}, f32[2048,64]{0,1:T(8,128)}, ...), condition=%wide.region_74.75_spmd.clone, body=%wide.region_72.74_spmd.clone.sunk | while | flops 684369408 | bytes 53651896 | solution.py:202
  961.7 6.6 multiply_reduce_fusion.20
  969.2 46.7 %while.176 = (s32[]{:T(128)}, f32[2048,64]{0,1:T(8,128)}, f32[2048,64]{0,1:T(8,128)}, f32[2,512,64]{1,0,2:T(2,128)}, s32[2]{0:T(128)S(1)}, /*index=5*/s32[1024]{...) while((s32[]{:T(128)}, f32[2048,64]{0,1:T(8,128)}, ...), condition=%wide.region_80.81_spmd.clone, body=%wide.region_78.80_spmd.clone.sunk | while | flops 684369408 | bytes 53684720 | solution.py:202
  1017.6 75.2 %while.171 = (s32[]{:T(128)}, f32[2048,64]{0,1:T(8,128)}, f32[2048,64]{0,1:T(8,128)}, f32[4,512,64]{1,2,0:T(8,128)}, s32[2048]{0:T(1024)S(1)}, /*index=5*/s32[4]...) while((s32[]{:T(128)}, f32[2048,64]{0,1:T(8,128)}, ...), condition=%wide.region_54.55_spmd.clone, body=%wide.region_52.54_spmd.clone.sunk | while | flops 684361216 | bytes 69905216 | solution.py:202
  1093.7 74.7 %while.172 = (s32[]{:T(128)}, f32[2048,64]{0,1:T(8,128)}, f32[2048,64]{0,1:T(8,128)}, f32[4,512,64]{1,2,0:T(8,128)}, s32[2048]{0:T(1024)S(1)}, /*index=5*/s32[4]...) while((s32[]{:T(128)}, f32[2048,64]{0,1:T(8,128)}, ...), condition=%wide.region_58.59_spmd.clone, body=%wide.region_56.58_spmd.clone.sunk | while | flops 684361216 | bytes 74099584 | solution.py:202
  1198.7 5.0 select_n.427
  1209.3 69.2 %while.173 = (s32[]{:T(128)}, f32[2048,64]{0,1:T(8,128)}, f32[2048,64]{0,1:T(8,128)S(1)}, f32[4,512,64]{1,2,0:T(8,128)}, s32[2048]{0:T(1024)S(1)}, /*index=5*/s3...) while((s32[]{:T(128)}, f32[2048,64]{0,1:T(8,128)}, ...), condition=%wide.region_62.63_spmd.clone, body=%wide.region_60.62_spmd.clone.sunk | while | flops 684361216 | bytes 69905224 | solution.py:202
  1292.5 5.8 broadcast_in_dim.413
  1301.2 3.8 fusion.246
  1314.8 5.7 reshape_reshape.64
  1323.6 5.7 fusion.132
  1331.9 5.8 broadcast_in_dim.420
  1343.0 5.8 broadcast_in_dim.422
  1351.6 4.9 fusion.154
  1363.0 7.0 fusion.283
  1370.1 6.8 convolution_bitcast_fusion
  1380.5 4.3 fusion.280
  1384.9 4.0 fusion.281
  1418.5 3.8 fusion.282
  1431.0 38.0 %all-reduce.26 = (f32[768]{0:T(1024)S(1)}, f32[768]{0:T(1024)S(1)}, f32[192]{0:T(256)S(1)}, f32[192]{0:T(256)S(1)}, f32[192]{0:T(256)S(1)}, /*index=5*/f32[192]{...) all-reduce(f32[768]{0:T(1024)S(1)} %get-tuple-element.1524, ...), channel_id=6, replica_groups=mesh['dp'=8,'tensor'=4] {'dp'}, use_global_device_ids=true, to_apply=%region_86.87.clone | all-reduce | flops 7680 | bytes 61440
  1473.6 6.4 all-reduce.27
  1483.1 19.7 %reduce-scatter.29.cloned.1.call-done = f32[96,768]{1,0:T(8,128)} async-done(((f32[768,768]{1,0:T(8,128)}), f32[96,768]{1,0:T(8,128)}) %reduce-scatter.29.cloned.1.call-update) | async-done | bytes 294928 | tf_op jit(solution)/shard_map/reduce_scatter | solution.py:514
  1502.8 73.3 %reduce-scatter.31.cloned.1.call-done = f32[96,768]{1,0:T(8,128)} async-done(((f32[768,768]{1,0:T(8,128)}), f32[96,768]{1,0:T(8,128)}) %reduce-scatter.31.cloned.1.call-update) | async-done | bytes 294928
  1576.2 66.3 %reduce-scatter.21.cloned.1.call-done = f32[96,192]{1,0:T(8,128)} async-done(((f32[768,192]{1,0:T(8,128)}), f32[96,192]{1,0:T(8,128)}) %reduce-scatter.21.cloned.1.call-update) | async-done | bytes 73744 | tf_op jit(solution)/shard_map/reduce_scatter | solution.py:510
  1642.5 66.2 %reduce-scatter.23.cloned.1.call-done = f32[96,192]{1,0:T(8,128)} async-done(((f32[768,192]{1,0:T(8,128)}), f32[96,192]{1,0:T(8,128)}) %reduce-scatter.23.cloned.1.call-update) | async-done | bytes 73744 | tf_op jit(solution)/shard_map/reduce_scatter | solution.py:511
  1708.7 66.1 %reduce-scatter.25.cloned.1.call-done = f32[96,192]{1,0:T(8,128)} async-done(((f32[768,192]{1,0:T(8,128)}), f32[96,192]{1,0:T(8,128)}) %reduce-scatter.25.cloned.1.call-update) | async-done | bytes 73744 | tf_op jit(solution)/shard_map/reduce_scatter | solution.py:512
  (1185 shorter events, 712.4 us)
Async XLA Ops:
  8.0 63.9 %copy-start.144 = (bf16[192,96]{1,0:T(8,128)(2,1)S(1)}, bf16[192,96]{1,0:T(8,128)(2,1)}, u32[]{:S(2)}) copy-start(bf16[192,96]{1,0:T(8,128)(2,1)} %param.56) | copy-start | bytes 110596
  8.0 64.0 %copy-start.185 = (s32[4]{0:T(128)S(1)}, s32[4]{0:T(128)}, u32[]{:S(2)}) copy-start(s32[4]{0:T(128)} %param.67) | copy-start | bytes 52
  8.0 66.6 %copy-start.141 = (bf16[96,192]{1,0:T(8,128)(2,1)S(1)}, bf16[96,192]{1,0:T(8,128)(2,1)}, u32[]{:S(2)}) copy-start(bf16[96,192]{1,0:T(8,128)(2,1)} %param.52) | copy-start | bytes 110596
  8.1 97.7 %copy-start.142 = (bf16[96,192]{1,0:T(8,128)(2,1)S(1)}, bf16[96,192]{1,0:T(8,128)(2,1)}, u32[]{:S(2)}) copy-start(bf16[96,192]{1,0:T(8,128)(2,1)} %param.51) | copy-start | bytes 110596
  8.1 128.6 %copy-start.143 = (bf16[96,192]{1,0:T(8,128)(2,1)S(1)}, bf16[96,192]{1,0:T(8,128)(2,1)}, u32[]{:S(2)}) copy-start(bf16[96,192]{1,0:T(8,128)(2,1)} %param.49) | copy-start | bytes 110596
  8.1 193.0 %all-gather.7.cloned.1.call-start = ((), (), s32[]{:S(2)}) async-start(), calls=%async_computation.10 | async-start | bytes 3932160 | tf_op jit(solution)/shard_map/all_gather | solution.py:35
  62.6 12.0 copy-start.145
  62.7 12.0 copy-start.147
  65.1 441.6 %reduce-scatter.13.cloned.1.call-start = ((), (), s32[]{:S(2)}) async-start(), calls=%async_computation.11 | async-start | bytes 7864320 | tf_op jit(solution)/shard_map/reduce_scatter | solution.py:39
  72.6 272.7 %copy-start.173 = (pred[3]{0:T(512)(128)(4,1)}, pred[3]{0:T(512)(128)(4,1)S(1)}, u32[]{:S(2)}) copy-start(pred[3]{0:T(512)(128)(4,1)S(1)} %broadcast_compare_fusion.12) | copy-start | bytes 13
  105.7 99.8 %copy-start.97 = (bf16[768,192]{1,0:T(8,128)(2,1)}, bf16[768,192]{1,0:T(8,128)(2,1)S(1)}, u32[]{:S(2)}) copy-start(bf16[768,192]{1,0:T(8,128)(2,1)S(1)} %all_gather.81) | copy-start | bytes 884740
  136.7 68.9 %copy-start.76 = (bf16[768,192]{1,0:T(8,128)(2,1)}, bf16[768,192]{1,0:T(8,128)(2,1)S(1)}, u32[]{:S(2)}) copy-start(bf16[768,192]{1,0:T(8,128)(2,1)S(1)} %all_gather.80) | copy-start | bytes 884740
  167.8 40.1 %copy-start.95 = (bf16[768,192]{1,0:T(8,128)(2,1)}, bf16[768,192]{1,0:T(8,128)(2,1)S(1)}, u32[]{:S(2)}) copy-start(bf16[768,192]{1,0:T(8,128)(2,1)S(1)} %all_gather.78) | copy-start | bytes 884740
  206.8 119.7 %collective-permute-start = (bf16[2048,384]{0,1:T(8,128)(2,1)}, bf16[2048,384]{0,1:T(8,128)(2,1)}, u32[]{:S(2)}, u32[]{:S(2)}) collective-permute-start(bf16[2048,384]{0,1:T(8,128)(2,1)} %pad_maximum_fusion.1), channel_id=1, source_target_pairs={{0,4},{4,0},{8,12},{12,8},{16,20},{20,16},{24,28},{28,24},{1,5},{5... | collective-permute-start | bytes 4718600 | tf_op jit(solution)/shard_map/ppermute | solution.py:22
  244.2 79.2 %copy-start.130 = (f32[4,512]{1,0:T(4,128)}, f32[4,512]{1,0:T(4,128)S(1)}, u32[]{:S(2)}) copy-start(f32[4,512]{1,0:T(4,128)S(1)} %get-tuple-element.753) | copy-start | bytes 24580
  277.0 46.4 %copy-start.131 = (f32[4,512]{1,0:T(4,128)}, f32[4,512]{1,0:T(4,128)S(1)}, u32[]{:S(2)}) copy-start(f32[4,512]{1,0:T(4,128)S(1)} %get-tuple-element.757) | copy-start | bytes 24580
  309.2 16.9 copy-start.132
  323.4 98.6 %copy-start.108 = (f32[1,4,4,128]{3,1,2,0:T(4,128)}, f32[1,4,4,128]{3,1,2,0:T(4,128)S(1)}, u32[]{:S(2)}) copy-start(f32[1,4,4,128]{3,1,2,0:T(4,128)S(1)} %copy.560) | copy-start | bytes 24580
  323.4 98.7 %copy-start.106 = (f32[1,4,4,128]{3,1,2,0:T(4,128)}, f32[1,4,4,128]{3,1,2,0:T(4,128)S(1)}, u32[]{:S(2)}) copy-start(f32[1,4,4,128]{3,1,2,0:T(4,128)S(1)} %copy.562) | copy-start | bytes 24580
  326.1 96.0 %copy-start.104 = (f32[1,4,4,128]{3,1,2,0:T(4,128)}, f32[1,4,4,128]{3,1,2,0:T(4,128)S(1)}, u32[]{:S(2)}) copy-start(f32[1,4,4,128]{3,1,2,0:T(4,128)S(1)} %copy.564) | copy-start | bytes 24580
  326.5 97.2 %copy-start.58 = (f32[4,512,64]{2,1,0:T(8,128)}, f32[4,512,64]{2,1,0:T(8,128)S(1)}, u32[]{:S(2)}) copy-start(f32[4,512,64]{2,1,0:T(8,128)S(1)} %copy.407) | copy-start | bytes 1572868
  372.6 49.5 %copy-start.129 = (f32[2048]{0:T(1024)}, f32[2048]{0:T(1024)S(1)}, u32[]{:S(2)}) copy-start(f32[2048]{0:T(1024)S(1)} %max.71) | copy-start | bytes 24580
  395.4 26.7 %copy-start.127 = (f32[2048]{0:T(1024)}, f32[2048]{0:T(1024)S(1)}, u32[]{:S(2)}) copy-start(f32[2048]{0:T(1024)S(1)} %max.75) | copy-start | bytes 24580
  401.7 20.4 %copy-start.164 = (pred[2048]{0:T(1024)(128)(4,1)S(1)}, pred[2048]{0:T(1024)(128)(4,1)}, u32[]{:S(2)}) copy-start(pred[2048]{0:T(1024)(128)(4,1)} %broadcast_in_dim.394) | copy-start | bytes 6148
  401.7 20.5 %copy-start.165 = (pred[2048]{0:T(1024)(128)(4,1)S(1)}, pred[2048]{0:T(1024)(128)(4,1)}, u32[]{:S(2)}) copy-start(pred[2048]{0:T(1024)(128)(4,1)} %broadcast_in_dim.398) | copy-start | bytes 6148
  401.7 20.5 %copy-start.166 = (pred[2048]{0:T(1024)(128)(4,1)S(1)}, pred[2048]{0:T(1024)(128)(4,1)}, u32[]{:S(2)}) copy-start(pred[2048]{0:T(1024)(128)(4,1)} %broadcast_in_dim.400) | copy-start | bytes 6148
  430.6 13.4 copy-start.78
  433.0 15.5 copy-start.54
  444.0 379.9 %copy-start.25 = (f32[2048,192]{0,1:T(8,128)}, f32[2048,192]{0,1:T(8,128)S(1)}, u32[]{:S(2)}) copy-start(f32[2048,192]{0,1:T(8,128)S(1)} %fusion.157) | copy-start | bytes 4718596
  448.5 65.8 %all-gather.13.cloned.1.call-start = ((), (), s32[]{:S(2)}) async-start(), calls=%async_computation.14 | async-start | bytes 1327104 | tf_op jit(solution)/shard_map/all_gather | solution.py:73
  449.1 73.8 %all-gather.15.cloned.1.call-start = ((), (), s32[]{:S(2)}) async-start(), calls=%async_computation.16 | async-start | bytes 3932160 | tf_op jit(solution)/shard_map/all_gather | solution.py:35
  449.7 116.7 %all-gather.11.cloned.1.call-start = ((), (), s32[]{:S(2)}) async-start(), calls=%async_computation.13 | async-start | bytes 1327104 | tf_op jit(solution)/shard_map/all_gather | solution.py:72
  450.3 145.1 %all-gather.9.cloned.1.call-start = ((), (), s32[]{:S(2)}) async-start(), calls=%async_computation.12 | async-start | bytes 3932160 | tf_op jit(solution)/shard_map/all_gather | solution.py:35
  510.6 218.1 %reduce-scatter.17.cloned.1.call-start = ((), (), s32[]{:S(2)}) async-start(), calls=%async_computation.17 | async-start | bytes 7864320 | tf_op jit(solution)/shard_map/reduce_scatter | solution.py:39
  648.8 15.0 copy-start.184
  668.6 121.4 %reduce-scatter.15.cloned.1.call-start = ((), (), s32[]{:S(2)}) async-start(), calls=%async_computation.15 | async-start | bytes 7864320 | tf_op jit(solution)/shard_map/reduce_scatter | solution.py:39
  676.9 147.1 %all-gather.17.cloned.1.call-start = ((), (), s32[]{:S(2)}) async-start(), calls=%async_computation.18 | async-start | bytes 3932160 | tf_op jit(solution)/shard_map/all_gather | solution.py:35
  795.3 12.2 copy-start.133
  795.3 620.2 %reduce-scatter.27.cloned.1.call-start = ((), (), s32[]{:S(2)}) async-start(), calls=%async_computation.23 | async-start | bytes 884736 | tf_op jit(solution)/shard_map/reduce_scatter | solution.py:513
  808.7 31.4 %copy-start.55 = (f32[2048,3,64]{0,2,1:T(8,128)S(1)}, f32[2048,3,64]{0,2,1:T(8,128)}, u32[]{:S(2)}) copy-start(f32[2048,3,64]{0,2,1:T(8,128)} %copy-done.54) | copy-start | bytes 4718596
  857.0 10.5 copy-start.189
  867.5 40.5 %copy-start.118 = (f32[1,4,2,128]{3,1,2,0:T(4,128)S(1)}, f32[1,4,2,128]{3,1,2,0:T(4,128)}, u32[]{:S(2)}) copy-start(f32[1,4,2,128]{3,1,2,0:T(4,128)} %copy-done.117) | copy-start | bytes 12292
  916.9 43.4 %copy-start.116 = (f32[1,4,2,128]{3,1,2,0:T(4,128)S(1)}, f32[1,4,2,128]{3,1,2,0:T(4,128)}, u32[]{:S(2)}) copy-start(f32[1,4,2,128]{3,1,2,0:T(4,128)} %copy-done.115) | copy-start | bytes 12292
  969.2 46.8 %copy-start.109 = (f32[1,4,4,128]{3,1,2,0:T(4,128)S(1)}, f32[1,4,4,128]{3,1,2,0:T(4,128)}, u32[]{:S(2)}) copy-start(f32[1,4,4,128]{3,1,2,0:T(4,128)} %copy-done.108) | copy-start | bytes 24580
  969.2 48.4 %copy-start.14 = (bf16[2048,64]{1,0:T(8,128)(2,1)S(1)}, bf16[2048,64]{1,0:T(8,128)(2,1)}, u32[]{:S(2)}) copy-start(bf16[2048,64]{1,0:T(8,128)(2,1)} %copy-done.13) | copy-start | bytes 786436
  969.2 48.4 %copy-start.57 = (s32[2048]{0:T(1024)S(1)}, s32[2048]{0:T(1024)}, u32[]{:S(2)}) copy-start(s32[2048]{0:T(1024)} %copy-done.56) | copy-start | bytes 24580
  1017.6 75.3 %copy-start.107 = (f32[1,4,4,128]{3,1,2,0:T(4,128)S(1)}, f32[1,4,4,128]{3,1,2,0:T(4,128)}, u32[]{:S(2)}) copy-start(f32[1,4,4,128]{3,1,2,0:T(4,128)} %copy-done.106) | copy-start | bytes 24580
  1017.6 75.3 %copy-start.128 = (f32[2048]{0:T(1024)S(1)}, f32[2048]{0:T(1024)}, u32[]{:S(2)}) copy-start(f32[2048]{0:T(1024)} %copy-done.127) | copy-start | bytes 24580
  1017.6 75.3 %copy-start.153 = (f32[2048]{0:T(1024)S(1)}, f32[2048]{0:T(1024)}, u32[]{:S(2)}) copy-start(f32[2048]{0:T(1024)} %get-tuple-element.1528) | copy-start | bytes 24580
  1017.6 75.3 %copy-start.167 = (pred[2048]{0:T(1024)(128)(4,1)S(1)}, pred[2048]{0:T(1024)(128)(4,1)}, u32[]{:S(2)}) copy-start(pred[2048]{0:T(1024)(128)(4,1)} %broadcast_in_dim.404) | copy-start | bytes 6148
  1017.6 76.1 %copy-start.12 = (bf16[2048,64]{1,0:T(8,128)(2,1)S(1)}, bf16[2048,64]{1,0:T(8,128)(2,1)}, u32[]{:S(2)}) copy-start(bf16[2048,64]{1,0:T(8,128)(2,1)} %copy-done.11) | copy-start | bytes 786436
  1198.7 10.5 copy-start.10
  1198.7 10.5 copy-start.21
  1198.7 10.5 copy-start.31
  1198.7 10.5 copy-start.187
  1206.8 104.7 %collective-permute-start.1 = (bf16[2048,384]{1,0:T(8,128)(2,1)}, bf16[2048,384]{1,0:T(8,128)(2,1)}, u32[]{:S(2)}, u32[]{:S(2)}) collective-permute-start(bf16[2048,384]{1,0:T(8,128)(2,1)} %pad_maximum_fusion.6), channel_id=1, source_target_pairs={{0,4},{4,0},{8,12},{12,8},{16,20},{20,16},{24,28},{28,24},{1,5},{5... | collective-permute-start | bytes 4718600 | tf_op jit(solution)/shard_map/ppermute | solution.py:22
  1209.2 69.2 %copy-start.103 = (f32[2,512,64]{1,0,2:T(2,128)S(1)}, f32[2,512,64]{1,0,2:T(2,128)}, u32[]{:S(2)}) copy-start(f32[2,512,64]{1,0,2:T(2,128)} %get-tuple-element.3539) | copy-start | bytes 786436
  1305.1 123.6 %reduce-scatter.19.cloned.1.call-start = ((), (), s32[]{:S(2)}) async-start(), calls=%async_computation.19 | async-start | bytes 7864320 | tf_op jit(solution)/shard_map/reduce_scatter | solution.py:39
  1362.7 140.1 %reduce-scatter.29.cloned.1.call-start = ((), (), s32[]{:S(2)}) async-start(), calls=%async_computation.24 | async-start | bytes 2654208 | tf_op jit(solution)/shard_map/reduce_scatter | solution.py:514
  1370.1 206.1 %reduce-scatter.31.cloned.1.call-start = ((), (), s32[]{:S(2)}) async-start(), calls=%async_computation.25 | async-start | bytes 2654208
  1380.5 262.0 %reduce-scatter.21.cloned.1.call-start = ((), (), s32[]{:S(2)}) async-start(), calls=%async_computation.20 | async-start | bytes 884736 | tf_op jit(solution)/shard_map/reduce_scatter | solution.py:510
  1384.9 323.9 %reduce-scatter.23.cloned.1.call-start = ((), (), s32[]{:S(2)}) async-start(), calls=%async_computation.21 | async-start | bytes 884736 | tf_op jit(solution)/shard_map/reduce_scatter | solution.py:511
  1388.9 385.9 %reduce-scatter.25.cloned.1.call-start = ((), (), s32[]{:S(2)}) async-start(), calls=%async_computation.22 | async-start | bytes 884736 | tf_op jit(solution)/shard_map/reduce_scatter | solution.py:512
  1422.5 57.6 %copy-start.68 = (f32[512,768]{1,0:T(8,128)S(1)}, f32[512,768]{1,0:T(8,128)}, u32[]{:S(2)}) copy-start(f32[512,768]{1,0:T(8,128)} %get-tuple-element.1864) | copy-start | bytes 4718596
  (199 other events, 839.6 us)
Sparse Core Ops, SparseCore 0:
  65.2 25.7 all-gather.6
  448.7 57.9 reduce-scatter.12
  795.4 28.4 all-gather.16
Sparse Core Ops, SparseCore 1:
  451.2 40.1 all-gather.12
  492.8 30.1 all-gather.14
  525.0 41.4 all-gather.10
  568.6 26.7 all-gather.8
  668.6 60.0 reduce-scatter.16
  731.2 58.7 reduce-scatter.14
  1305.2 63.3 reduce-scatter.26
  1371.0 57.7 reduce-scatter.18
  1432.7 70.1 reduce-scatter.28
  1506.9 69.2 reduce-scatter.30
  1579.9 62.5 reduce-scatter.20
  1646.4 62.3 reduce-scatter.22
  1712.5 62.3 reduce-scatter.24
where the time goes:
time: 1800 us; the launch traced here: 1780 us
  waiting for transfers between devices  540 us (30%)
  matrix products  342 us (19%)
  local copies, waits for them, and re-layouts  340 us (19%)
  blocking collectives  254 us (14%)
  other arithmetic  209 us (12%)
  loops' own time  72.9 us (4%)
  between operations  21.1 us (1%)
    dot_general x102, matrix products, contract(): lax.dot_general(left_side, right_side, (((left_dim,), (right_dim,)), ((),...  237 us
    reduce_scatter x4, waiting for transfers between devices, scatter_rows(): return lax.psum_scatter(values, 'tensor', scatter_dimension=0, tiled=True)  166 us
    unnamed x2, blocking collectives  77.5 us
    unnamed x17, waiting for transfers between devices  75.1 us
    reduce_scatter x1, waiting for transfers between devices, local(): lax.psum_scatter(grad_query_w, 'dp', scatter_dimension=0, tiled=True)  66.3 us
    reduce_scatter x1, waiting for transfers between devices, local(): lax.psum_scatter(grad_key_w, 'dp', scatter_dimension=0, tiled=True)  66.2 us
    reduce_scatter x1, waiting for transfers between devices, local(): lax.psum_scatter(grad_value_w, 'dp', scatter_dimension=0, tiled=True)  66.1 us
    unnamed x408, local copies, waits for them, and re-layouts  58.6 us
  transfers between devices with their start and end apart: 18, of which 13 were waited for; matrix products, arithmetic and copies ran while one was open for 20% of the time, Pallas kernels for 0%

commit v1 on v0

v1 whole, which is shorter than its diff:
```python
import math
from functools import partial

import jax
import jax.numpy as jnp
from jax import lax
from jax.experimental import pallas as pl
from jax.experimental.pallas import tpu as pltpu
from jax.sharding import PartitionSpec as P

epsilon = 1e-05
score_scale = 0.125
LOG2 = math.log(2.0)
CLOSED = -1e9
QB = 512


def mm(a, b):
    return jnp.dot(a, b, preferred_element_type=jnp.float32)


def flip(value):
    return value.astype(jnp.float32).T.astype(value.dtype)


def block_base(scal, base, rel, parity):
    return base + ((scal[0] ^ rel) << 9) + parity


def query_limit(scal, qb):
    lane = lax.broadcasted_iota(jnp.int32, (1, QB), 1)
    parity = qb // 2
    rel = (qb % 2) * 2
    low = block_base(scal, scal[1], rel, parity)
    high = block_base(scal, scal[1], rel + 1, parity)
    pos = 2 * (lane & 255) + jnp.where(lane < 256, low, high)
    return jnp.maximum(pos, scal[2] - 1)


def shut(s, scal, base, chunk, parity, limit):
    row = 2 * lax.broadcasted_iota(jnp.int32, (256, QB), 0)
    parts = []
    for sub in range(2):
        room = limit - block_base(scal, base, 2 * chunk + sub, parity)
        parts.append(jnp.where(row <= room, s[sub * 256 : sub * 256 + 256], CLOSED))
    return jnp.concatenate(parts, axis=0)


def near_fwd_kernel(scal, q_ref, k_ref, v_ref, o_ref, l_ref, k_nat, v_aug):
    head, qb = pl.program_id(0), pl.program_id(1)
    par = scal[4 + head]

    @pl.when(qb == 0)
    def _():
        k_nat[...] = flip(k_ref[...])
        v_aug[0:64] = v_ref[...]
        v_aug[64:80] = jnp.ones((16, 2048), jnp.bfloat16)

    far = qb // 2 == par

    def body(masked):
        q = q_ref[...]
        limit = query_limit(scal, qb)
        top = acc = None
        for c in range(4):
            s = mm(k_nat[c * 512 : c * 512 + 512], q)
            if masked:
                s = shut(s, scal, scal[1], c % 2, c // 2, limit)
            twice = jnp.where(far & (par == c // 2), LOG2, 0.0)
            peak = jnp.max(s, axis=0, keepdims=True)
            new = peak if c == 0 else jnp.maximum(top, peak)
            p = jnp.exp(s - (new - twice)).astype(jnp.bfloat16)
            part = mm(v_aug[:, c * 512 : c * 512 + 512], p)
            acc = part if c == 0 else acc * jnp.exp(top - new) + part
            top = new
        total = acc[64:65]
        o_ref[...] = acc[0:64] / total
        l_ref[0] = top + jnp.log(total)

    need = scal[2] < scal[1] + 2048
    pl.when(need)(lambda: body(True))
    pl.when(jnp.logical_not(need))(lambda: body(False))


def near_fwd(scal, q, k, v):
    return pl.pallas_call(
        near_fwd_kernel,
        grid_spec=pltpu.PrefetchScalarGridSpec(
            num_scalar_prefetch=1,
            grid=(3, 4),
            in_specs=[
                pl.BlockSpec((64, QB), lambda h, i, s: (h, i)),
                pl.BlockSpec((64, 2048), lambda h, i, s: (h, 0)),
                pl.BlockSpec((64, 2048), lambda h, i, s: (h, 0)),
            ],
            out_specs=[
                pl.BlockSpec((64, QB), lambda h, i, s: (h, i)),
                pl.BlockSpec((1, 1, QB), lambda h, i, s: (h, 0, i)),
            ],
            scratch_shapes=[
                pltpu.VMEM((2048, 64), jnp.bfloat16),
                pltpu.VMEM((80, 2048), jnp.bfloat16),
            ],
        ),
        out_shape=[
            jax.ShapeDtypeStruct((192, 2048), jnp.float32),
            jax.ShapeDtypeStruct((3, 1, 2048), jnp.float32),
        ],
        cost_estimate=pl.CostEstimate(flops=13000000000, bytes_accessed=4000000, transcendentals=12582912),
        name="near_fwd",
    )(scal, q, k, v)


def cross_fwd_kernel(scal, q_ref, k_ref, v_ref, o1_ref, l1_ref, o_ref, l_ref, k_nat, v_aug):
    head, qb = pl.program_id(0), pl.program_id(1)
    par = scal[4 + head]
    far = qb // 2 == par

    @pl.when(qb == 0)
    def _():
        k_nat[...] = flip(k_ref[...])
        v_aug[0:64] = v_ref[...]
        v_aug[64:80] = jnp.ones((16, 1024), jnp.bfloat16)

    @pl.when(jnp.logical_not(far))
    def _():
        o_ref[...] = o1_ref[...].astype(jnp.bfloat16)
        l_ref[...] = l1_ref[...]

    def body(masked):
        q = q_ref[...]
        limit = query_limit(scal, qb)
        top = acc = None
        for c in range(2):
            s = mm(k_nat[c * 512 : c * 512 + 512], q)
            if masked:
                s = shut(s, scal, scal[3], c, par, limit)
            peak = jnp.max(s, axis=0, keepdims=True)
            new = peak if c == 0 else jnp.maximum(top, peak)
            p = jnp.exp(s - new).astype(jnp.bfloat16)
            part = mm(v_aug[:, c * 512 : c * 512 + 512], p)
            acc = part if c == 0 else acc * jnp.exp(top - new) + part
            top = new
        l1 = l1_ref[0]
        new = jnp.maximum(l1, top)
        w1 = jnp.exp(l1 - new)
        w2 = jnp.exp(top - new)
        total = w1 + w2 * acc[64:65]
        o_ref[...] = ((w1 * o1_ref[...] + w2 * acc[0:64]) / total).astype(jnp.bfloat16)
        l_ref[0] = new + jnp.log(total)

    need = scal[3] > scal[1]
    pl.when(far & need)(lambda: body(True))
    pl.when(far & jnp.logical_not(need))(lambda: body(False))


def cross_fwd(scal, q, k, v, o1, l1):
    return pl.pallas_call(
        cross_fwd_kernel,
        grid_spec=pltpu.PrefetchScalarGridSpec(
            num_scalar_prefetch=1,
            grid=(3, 4),
            in_specs=[
                pl.BlockSpec((64, QB), lambda h, i, s: (h, i)),
                pl.BlockSpec((64, 1024), lambda h, i, s: (h, 0)),
                pl.BlockSpec((64, 1024), lambda h, i, s: (h + 3, 0)),
                pl.BlockSpec((64, QB), lambda h, i, s: (h, i)),
                pl.BlockSpec((1, 1, QB), lambda h, i, s: (h, 0, i)),
            ],
            out_specs=[
                pl.BlockSpec((64, QB), lambda h, i, s: (h, i)),
                pl.BlockSpec((1, 1, QB), lambda h, i, s: (h, 0, i)),
            ],
            scratch_shapes=[
                pltpu.VMEM((1024, 64), jnp.bfloat16),
                pltpu.VMEM((80, 1024), jnp.bfloat16),
            ],
        ),
        out_shape=[
            jax.ShapeDtypeStruct((192, 2048), jnp.bfloat16),
            jax.ShapeDtypeStruct((3, 1, 2048), jnp.float32),
        ],
        cost_estimate=pl.CostEstimate(flops=3300000000, bytes_accessed=4000000, transcendentals=3145728),
        name="cross_fwd",
    )(scal, q, k, v, o1, l1)


def back_chunk(masked_fn, k_c, v_c, kT_c, q, q_nat, do, do_nat, shift, delta):
    s = mm(k_c, q)
    if masked_fn is not None:
        s = masked_fn(s)
    p = jnp.exp(s - shift)
    dp = mm(v_c, do)
    ds = (p * (dp - delta)).astype(jnp.bfloat16)
    dv = mm(p.astype(jnp.bfloat16), do_nat)
    dk = mm(ds, q_nat)
    dq = mm(kT_c, ds)
    return dq, dk, dv


def near_bwd_kernel(scal, q_ref, k_ref, v_ref, do_ref, o_ref, l_ref, dq0_ref, dq_ref, dk_ref, dv_ref, k_nat, v_nat, dk_acc, dv_acc):
    head, qb = pl.program_id(0), pl.program_id(1)
    par = scal[4 + head]
    far = qb // 2 == par

    @pl.when(qb == 0)
    def _():
        k_nat[...] = flip(k_ref[...])
        v_nat[...] = flip(v_ref[...])
        dk_acc[...] = jnp.zeros_like(dk_acc)
        dv_acc[...] = jnp.zeros_like(dv_acc)

    def body(masked):
        q = q_ref[...]
        do = do_ref[...]
        q_nat, do_nat = flip(q), flip(do)
        delta = jnp.sum(do.astype(jnp.float32) * o_ref[...].astype(jnp.float32), axis=0, keepdims=True)
        limit = query_limit(scal, qb)
        dq = jnp.where(far, dq0_ref[...], 0.0)
        for c in range(4):
            rows = slice(c * 512, c * 512 + 512)
            twice = jnp.where(far & (par == c // 2), LOG2, 0.0)
            masking = (lambda s: shut(s, scal, scal[1], c % 2, c // 2, limit)) if masked else None
            gq, gk, gv = back_chunk(
                masking, k_nat[rows], v_nat[rows], k_ref[:, rows], q, q_nat, do, do_nat, l_ref[0] - twice, delta
            )
            dq = dq + gq
            dk_acc[rows] += gk
            dv_acc[rows] += gv
        dq_ref[...] = (dq * 0.125).astype(jnp.bfloat16)

    need = scal[2] < scal[1] + 2048
    pl.when(need)(lambda: body(True))
    pl.when(jnp.logical_not(need))(lambda: body(False))

    @pl.when(qb == 3)
    def _():
        dk_ref[...] = dk_acc[...].T
        dv_ref[...] = dv_acc[...].T


def far_block(i, par):
    return jnp.clip(i - 2 * par, 0, 1)


def near_bwd(scal, q, k, v, do, o, l, dq0):
    full = pl.BlockSpec((64, 2048), lambda h, i, s: (h, 0))
    part = pl.BlockSpec((64, QB), lambda h, i, s: (h, i))
    return pl.pallas_call(
        near_bwd_kernel,
        grid_spec=pltpu.PrefetchScalarGridSpec(
            num_scalar_prefetch=1,
            grid=(3, 4),
            in_specs=[
                part,
                full,
                full,
                part,
                part,
                pl.BlockSpec((1, 1, QB), lambda h, i, s: (h, 0, i)),
                pl.BlockSpec((64, QB), lambda h, i, s: (h, far_block(i, s[4 + h]))),
            ],
            out_specs=[part, full, full],
            scratch_shapes=[
                pltpu.VMEM((2048, 64), jnp.bfloat16),
                pltpu.VMEM((2048, 64), jnp.bfloat16),
                pltpu.VMEM((2048, 64), jnp.float32),
                pltpu.VMEM((2048, 64), jnp.float32),
            ],
        ),
        out_shape=[
            jax.ShapeDtypeStruct((192, 2048), jnp.bfloat16),
            jax.ShapeDtypeStruct((192, 2048), jnp.float32),
            jax.ShapeDtypeStruct((192, 2048), jnp.float32),
        ],
        cost_estimate=pl.CostEstimate(flops=32000000000, bytes_accessed=8000000, transcendentals=12582912),
        name="near_bwd",
    )(scal, q, k, v, do, o, l, dq0)


def cross_bwd_kernel(scal, q_ref, k_ref, v_ref, do_ref, o_ref, l_ref, dq_ref, dk_ref, dv_ref, k_nat, v_nat, dk_acc, dv_acc):
    head, i = pl.program_id(0), pl.program_id(1)
    par = scal[4 + head]

    @pl.when(i == 0)
    def _():
        k_nat[...] = flip(k_ref[...])
        v_nat[...] = flip(v_ref[...])
        dk_acc[...] = jnp.zeros_like(dk_acc)
        dv_acc[...] = jnp.zeros_like(dv_acc)

    def body(masked):
        q = q_ref[...]
        do = do_ref[...]
        q_nat, do_nat = flip(q), flip(do)
        delta = jnp.sum(do.astype(jnp.float32) * o_ref[...].astype(jnp.float32), axis=0, keepdims=True)
        limit = query_limit(scal, i + 2 * par)
        dq = None
        for c in range(2):
            rows = slice(c * 512, c * 512 + 512)
            masking = (lambda s: shut(s, scal, scal[3], c, par, limit)) if masked else None
            gq, gk, gv = back_chunk(
                masking, k_nat[rows], v_nat[rows], k_ref[:, rows], q, q_nat, do, do_nat, l_ref[0], delta
            )
            dq = gq if c == 0 else dq + gq
            dk_acc[rows] += gk
            dv_acc[rows] += gv
        dq_ref[...] = dq

    need = scal[3] > scal[1]
    pl.when(need)(lambda: body(True))
    pl.when(jnp.logical_not(need))(lambda: body(False))

    @pl.when(i == 1)
    def _():
        dk_ref[...] = dk_acc[...].T.astype(jnp.bfloat16)
        dv_ref[...] = dv_acc[...].T.astype(jnp.bfloat16)


def cross_bwd(scal, q, kv, do, o, l):
    part = pl.BlockSpec((64, QB), lambda h, i, s: (h, i + 2 * s[4 + h]))
    full = pl.BlockSpec((64, 1024), lambda h, i, s: (h, 0))
    return pl.pallas_call(
        cross_bwd_kernel,
        grid_spec=pltpu.PrefetchScalarGridSpec(
            num_scalar_prefetch=1,
            grid=(3, 2),
            in_specs=[
                part,
                full,
                pl.BlockSpec((64, 1024), lambda h, i, s: (h + 3, 0)),
                part,
                part,
                pl.BlockSpec((1, 1, QB), lambda h, i, s: (h, 0, i + 2 * s[4 + h])),
            ],
            out_specs=[pl.BlockSpec((64, QB), lambda h, i, s: (h, i)), full, full],
            scratch_shapes=[
                pltpu.VMEM((1024, 64), jnp.bfloat16),
                pltpu.VMEM((1024, 64), jnp.bfloat16),
                pltpu.VMEM((1024, 64), jnp.float32),
                pltpu.VMEM((1024, 64), jnp.float32),
            ],
        ),
        out_shape=[
            jax.ShapeDtypeStruct((192, 1024), jnp.float32),
            jax.ShapeDtypeStruct((192, 1024), jnp.bfloat16),
            jax.ShapeDtypeStruct((192, 1024), jnp.bfloat16),
        ],
        cost_estimate=pl.CostEstimate(flops=8000000000, bytes_accessed=6000000, transcendentals=3145728),
        name="cross_bwd",
    )(scal, q, kv, kv, do, o, l)


def contract(left_side, right_side, left_dim, right_dim):
    return lax.dot_general(
        left_side,
        right_side,
        (((left_dim,), (right_dim,)), ((), ())),
        preferred_element_type=jnp.float32,
    )


def swap(value, axis, mask):
    pairs = [(source, source ^ mask) for source in range(lax.axis_size(axis))]
    return lax.ppermute(value, axis, pairs)


def assemble_kernel(where_ref, *refs):
    pieces, full_ref, rows_ref = refs[:-2], refs[-2], refs[-1]
    rows = full_ref.shape[0] // len(pieces)
    for k, piece in enumerate(pieces):
        owner = where_ref[0] ^ k
        full_ref[pl.ds(pl.multiple_of(owner * rows, rows), rows), :] = piece[0:rows, :]
        rows_ref[pl.ds(owner, 1), :] = piece[rows : rows + 1, :].astype(jnp.float32)


def gather_dp(shard, extra, place):
    size = lax.axis_size("dp")
    rows, columns = shard.shape
    if rows % 16:
        return (
            lax.all_gather(shard, "dp", axis=0, tiled=True),
            lax.all_gather(extra, "dp", axis=0, tiled=False).astype(jnp.float32),
        )
    packed = jnp.concatenate((shard, jnp.pad(extra[None, :], ((0, 15), (0, 0)))), axis=0)
    pieces = [packed] + [swap(packed, "dp", mask) for mask in range(1, size)]
    whole = pl.BlockSpec(memory_space=pltpu.VMEM)
    return pl.pallas_call(
        assemble_kernel,
        in_specs=[pl.BlockSpec(memory_space=pltpu.SMEM)] + [whole] * size,
        out_specs=[whole, whole],
        out_shape=[
            jax.ShapeDtypeStruct((size * rows, columns), shard.dtype),
            jax.ShapeDtypeStruct((size, columns), jnp.float32),
        ],
        name="assemble",
    )(place[None], *pieces)


def reduce_dp(values, place):
    size = lax.axis_size("dp")
    rows = values.shape[0] // size
    if size > 8:
        return lax.psum_scatter(values.astype(jnp.float32), "dp", scatter_dimension=0, tiled=True)
    total = lax.dynamic_slice_in_dim(values, place * rows, rows).astype(jnp.float32)
    for mask in range(1, size):
        piece = lax.dynamic_slice_in_dim(values, (place ^ mask) * rows, rows)
        total = total + swap(piece, "dp", mask).astype(jnp.float32)
    return total


def norm_rows(values, axis):
    middle_point = jnp.mean(values, axis=axis, keepdims=True)
    spread = jnp.mean(values * values, axis=axis, keepdims=True) - middle_point * middle_point
    scaling = lax.rsqrt(spread + epsilon)
    return (values - middle_point) * scaling, scaling


def norm_back(grad_hat, normed, scaling, axis):
    return scaling * (
        grad_hat
        - jnp.mean(grad_hat, axis=axis, keepdims=True)
        - normed * jnp.mean(grad_hat * normed, axis=axis, keepdims=True)
    )


def split_parity(rows):
    return rows.reshape(256, 2, -1).transpose(1, 0, 2).reshape(512, -1)


def join_parity(rows):
    return rows.reshape(2, 256, -1).transpose(1, 0, 2).reshape(512, -1)


def halves(value):
    upper = value.astype(jnp.bfloat16)
    return upper, (value - upper.astype(jnp.float32)).astype(jnp.bfloat16)


def local(
    layer_in,
    ln1_gain,
    ln1_bias,
    query_weight,
    query_bias,
    key_weight,
    value_weight,
    value_bias,
    inner_gain,
    inner_bias,
    output_weight,
    output_bias,
    ln2_gain,
    ln2_bias,
    up_weight,
    up_bias,
    outer_gain,
    outer_bias,
    down_weight,
    down_bias,
    out_grad,
    prefix,
):
    size = lax.axis_size("dp")
    place = lax.axis_index("dp")
    member = lax.axis_index("tensor")
    rows = 768 // size
    small = 192 // size
    base = place % 2 * 2048
    prefix_len = lax.dynamic_index_in_dim(prefix, place // 2, keepdims=False)
    parities = [(member * 3 + head) % 2 for head in range(3)]
    scal = jnp.stack([member, base, prefix_len, 2048 - base] + parities).astype(jnp.int32)
    parity_rows = jnp.repeat((member * 3 + jnp.arange(3, dtype=jnp.int32)) % 2, 64)[:, None]

    mine = split_parity(layer_in)
    from_core = swap(mine, "tensor", 1)
    from_chip = swap(mine, "tensor", 2)
    from_both = swap(from_chip, "tensor", 1)
    quarters = (mine, from_core, from_chip, from_both)
    segment = jnp.concatenate([q[:256] for q in quarters] + [q[256:] for q in quarters], axis=0)

    qkv_shard = jnp.concatenate((query_weight, key_weight, value_weight), axis=1)
    qkv_extra = jnp.concatenate((ln1_gain, ln1_bias, query_bias, value_bias))
    qkv_extra = jnp.pad(qkv_extra, (0, 576 - qkv_extra.shape[0]))
    qkv_full, qkv_rows = gather_dp(qkv_shard, qkv_extra, place)
    norm1_scale = qkv_rows[:, :rows].reshape(768)
    norm1_shift = qkv_rows[:, rows : 2 * rows].reshape(768)
    query_shift = qkv_rows[:, 2 * rows : 2 * rows + small].reshape(192)
    value_shift = qkv_rows[:, 2 * rows + small : 2 * rows + 2 * small].reshape(192)

    vectors = jnp.concatenate(
        (output_bias, ln2_gain, ln2_bias, down_bias, up_bias, outer_gain, outer_bias, inner_gain, inner_bias)
    )
    wide_shard = jnp.concatenate((up_weight, down_weight.T, output_weight.T), axis=1)
    wide_shard = jnp.concatenate((wide_shard, jnp.pad(vectors, (0, 1728 - vectors.shape[0]))[None]), axis=0)
    wide_shard = jnp.pad(wide_shard, ((0, -(rows + 1) % 16), (0, 0)))
    wide = lax.all_gather(wide_shard, ("dp", "tensor"), axis=0, tiled=False)
    wide = wide.reshape(size, 4, wide_shard.shape[0], 1728)
    blocks = [lax.dynamic_index_in_dim(wide, member ^ k, axis=1, keepdims=False) for k in range(4)]

    def columns_of(start, stop):
        return jnp.concatenate([b[:, :rows, start:stop].reshape(768, stop - start) for b in blocks], axis=1)

    up_full = columns_of(0, 768)
    down_flip = columns_of(768, 1536)
    output_flip = columns_of(1536, 1728)
    lines = [b[:, rows].astype(jnp.float32) for b in blocks]
    same = lines[0][:, : 4 * rows].reshape(size, 4, rows).transpose(1, 0, 2).reshape(4, 768)
    output_shift, norm2_scale, norm2_shift, down_shift = same[0], same[1], same[2], same[3]
    per_unit = [
        line[:, 4 * rows : 7 * rows].reshape(size, 3, rows).transpose(1, 0, 2).reshape(3, 768) for line in lines
    ]
    units = jnp.concatenate(per_unit, axis=1)
    up_shift, outer_scale, outer_shift = units[0], units[1], units[2]
    per_head = [
        line[:, 7 * rows : 7 * rows + 2 * small].reshape(size, 2, small).transpose(1, 0, 2).reshape(2, 192)
        for line in lines
    ]
    head_rows = jnp.concatenate(per_head, axis=1)
    inner_scale, inner_shift = head_rows[0][:, None], head_rows[1][:, None]

    hat_segment, _ = norm_rows(segment.astype(jnp.float32), 1)
    hidden_one = (hat_segment * norm1_scale + norm1_shift).astype(jnp.bfloat16)
    shifts = jnp.concatenate((query_shift, jnp.zeros(192, jnp.float32), value_shift))[:, None]
    projected = (contract(qkv_full, hidden_one, 0, 1) + shifts).astype(jnp.bfloat16)
    query = projected[:192] * jnp.bfloat16(score_scale)
    key, value = projected[192:384], projected[384:]
    both_rows = jnp.concatenate((parity_rows, parity_rows), axis=0)
    far_own = jnp.where(both_rows == 1, projected[192:, 1024:], projected[192:, :1024])
    far_other = swap(far_own, "dp", 1)
    near_out, near_log = near_fwd(scal, query, key, value)
    attended, log_total = cross_fwd(scal, query, far_other, far_other, near_out, near_log)

    by_row = attended.reshape(192, 2, 4, 256)
    got = swap(by_row[:, :, 2:], "tensor", 2)
    pair = jnp.stack((by_row[:, :, :2], got), axis=0)
    got = swap(pair[:, :, :, 1], "tensor", 1)
    kept = pair[:, :, :, 0]
    heads = jnp.concatenate((kept[0], got[0], kept[1], got[1]), axis=0).reshape(768, 512)

    inner_hat, inner_scaling = norm_rows(heads.astype(jnp.float32), 0)
    inner_rows = (inner_hat * inner_scale + inner_shift).astype(jnp.bfloat16)
    layer_float = mine.astype(jnp.float32)
    middle = layer_float + contract(inner_rows, output_flip, 0, 1) + output_shift
    hat_two, scale_two = norm_rows(middle, 1)
    hidden_two = (hat_two * norm2_scale + norm2_shift).astype(jnp.bfloat16)
    up_rows = jnp.dot(hidden_two, up_full, preferred_element_type=jnp.float32) + up_shift
    activated, gelu_back = jax.vjp(partial(jax.nn.gelu, approximate=False), up_rows)
    outer_hat, outer_scaling = norm_rows(activated, 1)
    outer_rows = (outer_hat * outer_scale + outer_shift).astype(jnp.bfloat16)
    layer_out = middle + contract(outer_rows, down_flip, 1, 1) + down_shift

    grad_low = split_parity(out_grad)
    grad_float = grad_low.astype(jnp.float32)
    grad_down_flip = contract(grad_low, outer_rows, 0, 0)
    outer_grad = jnp.dot(grad_low, down_flip, preferred_element_type=jnp.float32)
    grad_outer_scale = jnp.sum(outer_grad * outer_hat, axis=0)
    grad_outer_shift = jnp.sum(outer_grad, axis=0)
    up_grad = gelu_back(norm_back(outer_grad * outer_scale, outer_hat, outer_scaling, 1))[0].astype(jnp.bfloat16)
    grad_up_shift = jnp.sum(up_grad.astype(jnp.float32), axis=0)
    grad_up = contract(hidden_two, up_grad, 0, 0)
    hidden_two_grad = contract(up_grad, up_full, 1, 1)
    grad_norm2_scale = jnp.sum(hidden_two_grad * hat_two, axis=0)
    grad_norm2_shift = jnp.sum(hidden_two_grad, axis=0)
    middle_grad = grad_float + norm_back(hidden_two_grad * norm2_scale, hat_two, scale_two, 1)
    middle_low = middle_grad.astype(jnp.bfloat16)
    grad_output_shift = jnp.sum(middle_low.astype(jnp.float32), axis=0)
    grad_down_shift = jnp.sum(grad_float, axis=0)
    grad_output_flip = contract(middle_low, inner_rows, 0, 1)
    inner_grad = contract(output_flip, middle_low, 0, 1)
    grad_inner_scale = jnp.sum(inner_grad * inner_hat, axis=1)
    grad_inner_shift = jnp.sum(inner_grad, axis=1)
    heads_grad = norm_back(inner_grad * inner_scale, inner_hat, inner_scaling, 0).astype(jnp.bfloat16)

    split = heads_grad.reshape(4, 192, 2, 256)
    got = swap(jnp.stack((split[1], split[3])), "tensor", 1)
    sent = jnp.stack((split[2], got[1]), axis=2)
    got_chip = swap(sent, "tensor", 2)
    attended_grad = jnp.concatenate(
        (jnp.stack((split[0], got[0]), axis=2), got_chip), axis=2
    ).reshape(192, 2048)

    query_first, far_key_grad, far_value_grad = cross_bwd(scal, query, far_other, attended_grad, attended, log_total)
    returned = swap(jnp.concatenate((far_key_grad, far_value_grad), axis=0), "dp", 1)
    query_low, key_near, value_near = near_bwd(
        scal, query, key, value, attended_grad, attended, log_total, query_first
    )
    side = (jnp.arange(2, dtype=jnp.int32)[None, :] == both_rows)[:, :, None]
    spread_far = jnp.where(side, returned.astype(jnp.float32)[:, None, :], 0.0).reshape(384, 2048)
    key_value_low = (jnp.concatenate((key_near, value_near), axis=0) + spread_far).astype(jnp.bfloat16)
    all_low = jnp.concatenate((query_low, key_value_low), axis=0)
    column_sums = jnp.sum(all_low.astype(jnp.float32), axis=1)

    def pad_small(vector):
        return jnp.pad(vector.reshape(4, size, small), ((0, 0), (0, 0), (0, rows - small))).reshape(4, 768)

    repeated = jnp.stack((grad_output_shift, grad_norm2_scale, grad_norm2_shift, grad_down_shift))
    unit_columns = jnp.stack((grad_up_shift, grad_outer_scale, grad_outer_shift)).reshape(3, 4, 768)
    head_columns = jnp.stack((pad_small(grad_inner_scale), pad_small(grad_inner_shift)))
    extra = jnp.concatenate((jnp.broadcast_to(repeated[:, None], (4, 4, 768)), unit_columns, head_columns), axis=0)
    extra = jnp.pad(extra.transpose(1, 2, 0), ((0, 0), (0, 0), (0, 55))).astype(jnp.bfloat16)

    def wide_block(k):
        return jnp.concatenate(
            (
                grad_up[:, k * 768 : k * 768 + 768].astype(jnp.bfloat16),
                grad_down_flip[:, k * 768 : k * 768 + 768].astype(jnp.bfloat16),
                grad_output_flip[:, k * 192 : k * 192 + 192].astype(jnp.bfloat16),
                extra[k],
            ),
            axis=1,
        )

    got_first = swap(wide_block(3), "tensor", 1)
    got_second = swap(wide_block(1), "tensor", 1)
    to_chip = (wide_block(2).astype(jnp.float32) + got_first.astype(jnp.float32)).astype(jnp.bfloat16)
    from_other = swap(to_chip, "tensor", 2)
    wide_sum = (
        wide_block(0).astype(jnp.float32) + got_second.astype(jnp.float32) + from_other.astype(jnp.float32)
    ).astype(jnp.bfloat16)
    wide_own = reduce_dp(wide_sum, place)

    partial_rows = contract(all_low, qkv_full, 0, 1).reshape(2, 4, 256, 768)
    got = swap(jnp.stack((partial_rows[:, 1], partial_rows[:, 3])).astype(jnp.bfloat16), "tensor", 1)
    got = got.astype(jnp.float32)
    got_chip = swap((partial_rows[:, 2] + got[1]).astype(jnp.bfloat16), "tensor", 2)
    hidden_one_grad = (partial_rows[:, 0] + got[0] + got_chip.astype(jnp.float32)).reshape(512, 768)

    grad_qkv = contract(hidden_one, all_low, 0, 1)
    full_float = qkv_full.astype(jnp.float32)
    along = jnp.sum(full_float * grad_qkv, axis=1)
    shift_part = jnp.sum(full_float * column_sums[None, :], axis=1)

    def small_column(vector):
        return jnp.pad(vector.reshape(size, small), ((0, 0), (0, rows - small))).reshape(768)

    columns = [*halves(along), *halves(shift_part)]
    columns += [*halves(small_column(column_sums[:192])), *halves(small_column(column_sums[384:]))]
    qkv_grads = jnp.concatenate(
        (grad_qkv.astype(jnp.bfloat16), jnp.pad(jnp.stack(columns, axis=1), ((0, 0), (0, 56)))), axis=1
    )
    qkv_own = reduce_dp(qkv_grads, place)
    norm_pair = jnp.stack((qkv_own[:, 576] + qkv_own[:, 577], qkv_own[:, 578] + qkv_own[:, 579]))
    norm_pair = norm_pair + swap(norm_pair, "tensor", 1)
    norm_pair = norm_pair + swap(norm_pair, "tensor", 2)
    gain_own, bias_own = ln1_gain.astype(jnp.float32), ln1_bias.astype(jnp.float32)
    grad_ln1_gain = (norm_pair[0] - bias_own * norm_pair[1]) / gain_own

    hat_one, scale_one = norm_rows(layer_float, 1)
    input_grad = middle_grad + norm_back(hidden_one_grad * norm1_scale, hat_one, scale_one, 1)

    return (
        join_parity(layer_out.astype(jnp.bfloat16)),
        join_parity(input_grad),
        grad_ln1_gain,
        norm_pair[1],
        qkv_own[:, :192],
        qkv_own[:small, 580] + qkv_own[:small, 581],
        qkv_own[:, 192:384],
        qkv_own[:, 384:576],
        qkv_own[:small, 582] + qkv_own[:small, 583],
        wide_own[:small, 1735],
        wide_own[:small, 1736],
        wide_own[:, 1536:1728].T,
        wide_own[:, 1728],
        wide_own[:, 1729],
        wide_own[:, 1730],
        wide_own[:, :768],
        wide_own[:, 1732],
        wide_own[:, 1733],
        wide_own[:, 1734],
        wide_own[:, 768:1536].T,
        wide_own[:, 1731],
    )


def solution(mesh):
    in_specs = (
        P(("dp", "tensor"), None),
        P("dp"),
        P("dp"),
        P("dp", "tensor"),
        P(("tensor", "dp")),
        P("dp", "tensor"),
        P("dp", "tensor"),
        P(("tensor", "dp")),
        P(("tensor", "dp")),
        P(("tensor", "dp")),
        P("tensor", "dp"),
        P("dp"),
        P("dp"),
        P("dp"),
        P("dp", "tensor"),
        P(("tensor", "dp")),
        P(("tensor", "dp")),
        P(("tensor", "dp")),
        P("tensor", "dp"),
        P("dp"),
        P(("dp", "tensor"), None),
        P(),
    )
    out_specs = (
        P(("dp", "tensor"), None),
        P(("dp", "tensor"), None),
        P("dp"),
        P("dp"),
        P("dp", "tensor"),
        P(("tensor", "dp")),
        P("dp", "tensor"),
        P("dp", "tensor"),
        P(("tensor", "dp")),
        P(("tensor", "dp")),
        P(("tensor", "dp")),
        P("tensor", "dp"),
        P("dp"),
        P("dp"),
        P("dp"),
        P("dp", "tensor"),
        P(("tensor", "dp")),
        P(("tensor", "dp")),
        P(("tensor", "dp")),
        P("tensor", "dp"),
        P("dp"),
    )
    return jax.shard_map(local, mesh=mesh, in_specs=in_specs, out_specs=out_specs, check_vma=False)
```

time: 1800 us -> 605 us (0.34)
  waiting for transfers between devices: 540 us -> 110 us
  matrix products: 342 us -> 65.1 us
  blocking collectives: 254 us -> 0 us
  local copies, waits for them, and re-layouts: 340 us -> 146 us
  other arithmetic: 209 us -> 63.3 us
  Pallas kernels: 0 us -> 98 us
  starting transfers between devices: 2.72 us -> 94.4 us
  loops' own time: 72.9 us -> 0 us
    reduce_scatter x9 -> x0, waiting for transfers between devices: 384 us -> none  [the longest x4 166 us: scatter_rows(): return lax.psum_scatter(values, 'tensor', scatter_dimension=0, tiled=True)]
    dot_general x102 -> x10, matrix products: 237 us -> 35.7 us  [contract(): lax.dot_general(left_side, right_side, (((left_dim,), (right_dim,)), ((),...]
    all_gather x4 -> x0, blocking collectives: 126 us -> none  [the longest x1 33.4 us: fetch_first(): lax.all_gather(output_flip, 'dp', axis=0, tiled=True)]
    ppermute x2 -> x37, waiting for transfers between devices: 0.01 us -> 110 us  [swap(): return lax.ppermute(value, axis, pairs)]
    pallas_call x0 -> x5, Pallas kernels: none -> 98 us  [the longest x1 40.9 us: near_bwd(): pl.pallas_call(near_bwd_kernel, grid_spec=pltpu.PrefetchScalarGridSpec(nu...]
    ppermute x2 -> x37, starting transfers between devices: 1.57 us -> 94.4 us  [swap(): return lax.ppermute(value, axis, pairs)]
    all_gather x6 -> x1, waiting for transfers between devices: 81.3 us -> 0.01 us  [local(): wide = lax.all_gather(wide_shard, ('dp', 'tensor'), axis=0, tiled=False)]
    unnamed x2 -> x0, blocking collectives: 77.5 us -> none
  transfers between devices with their start and end apart: 18 -> 38, of which waited for: 13 -> 13; matrix products, arithmetic and copies ran while one was open for 20% -> 22% of each run, Pallas kernels for 0% -> 17%
where the time goes in v1:
time: 605 us; the launch traced here: 593 us
  local copies, waits for them, and re-layouts  146 us (24%)
  waiting for transfers between devices  110 us (18%)
  Pallas kernels  98 us (16%)
  starting transfers between devices  94.4 us (16%)
  matrix products  65.1 us (11%)
  other arithmetic  63.3 us (10%)
  between operations  16.3 us (3%)
    ppermute x37, waiting for transfers between devices, swap(): return lax.ppermute(value, axis, pairs)  110 us
    ppermute x37, starting transfers between devices, swap(): return lax.ppermute(value, axis, pairs)  94.4 us
    pallas_call x1, Pallas kernels, near_bwd(): pl.pallas_call(near_bwd_kernel, grid_spec=pltpu.PrefetchScalarGridSpec(nu...  40.9 us
    dot_general x10, matrix products, contract(): lax.dot_general(left_side, right_side, (((left_dim,), (right_dim,)), ((),...  35.7 us
    pallas_call x1, Pallas kernels, near_fwd(): pl.pallas_call(near_fwd_kernel, grid_spec=pltpu.PrefetchScalarGridSpec(nu...  27.2 us
    unnamed x233, local copies, waits for them, and re-layouts  21.4 us
    dot_general x1, matrix products, local(): jnp.dot(hidden_two, up_full, preferred_element_type=jnp.float32) + up_shift  21.1 us
    concatenate x4, local copies, waits for them, and re-layouts, wide_block(): jnp.concatenate((grad_up[:, k * 768:k * 768 + 768].astype(jnp.bfloat16),...  17.9 us
  transfers between devices with their start and end apart: 38, of which 13 were waited for; matrix products, arithmetic and copies ran while one was open for 22% of the time, Pallas kernels for 17%

profile of v1, /device:TPU:0, one launch (start us, length us, event | category | flops | bytes accessed | tf_op | source)
XLA Modules:
  0.0 593.1 jit_solution(5268301253235930824)
XLA Ops:
  7.3 6.1 %concatenate.113 = bf16[720]{0:T(1024)(128)(2,1)S(1)} concatenate(bf16[96]{0:T(256)(128)(2,1)} %param.33, bf16[96]{0:T(256)(128)(2,1)} %param.34, bf16[96]{0:T(256)(128)(2,1)} %param.35, bf16[96]{0:T(256)(128)(2,1)} %param.41, bf16[96]{0:T(256)(128)(2,1)} %param.37, bf16[96]{0:T(256)(128)(2,1)} %param.38, bf16[96]{0:T(256)(128)(2,1)} %param.39, bf16[24]{0:T(256)(128)(2,1)} %param.30, ...), dimensions={0} | concatenate | bytes 2880 | tf_op jit(solution)/shard_map/concatenate | solution.py:491
  16.1 2.2 reshape.620
  18.4 3.0 collective-permute-start.8
  21.7 4.6 collective-permute-start.6
  30.2 2.3 collective-permute-done.6.refs_7_
  32.5 16.5 %collective-permute-start.2 = (bf16[112,576]{1,0:T(8,128)(2,1)S(1)}, bf16[112,576]{1,0:T(8,128)(2,1)}, u32[]{:S(2)}, u32[]{:S(2)}) collective-permute-start(bf16[112,576]{1,0:T(8,128)(2,1)S(1)} %fusion.68.refs_0_), channel_id=1, source_target_pairs={{0,12},{4,8},{8,4},{12,0},{16,28},{20,24},{24,20},{28,16},{1,13},{... | collective-permute-start | bytes 387080 | tf_op jit(solution)/shard_map/ppermute | solution.py:365
  49.0 5.3 collective-permute-start.1
  54.3 2.6 collective-permute-done.4.refs_5_
  61.2 8.2 %collective-permute-done.1.refs_2_ = bf16[112,576]{1,0:T(8,128)(2,1)} collective-permute-done((bf16[112,576]{1,0:T(8,128)(2,1)S(1)}, bf16[112,576]{1,0:T(8,128)(2,1)}, u32[]{:S(2)}, u32[]{:S(2)}) %collective-permute-start.1) | collective-permute-done | bytes 129056 | tf_op jit(solution)/shard_map/ppermute | solution.py:365
  69.4 2.4 assemble.1
  81.4 3.0 convert_reduce_fusion
  84.5 3.6 add_convert_fusion.4
  90.9 27.2 %near_fwd.1 = (f32[192,2048]{1,0:T(8,128)}, f32[3,1,2048]{2,1,0:T(1,128)}) custom-call(s32[7]{0:T(128)} %stack.88.scal, bf16[192,2048]{1,0:T(8,128)(2,1)} %get-tuple-element.210.q_ref, bf16[192,2048]{1,0:T(8,128)(2,1)} %get-tuple-element.209.k_ref, bf16[192,2048]{1,0:T(8,128)(2,1)} %get-tuple-element.208.v_ref), custom_call_target="tpu_custom_call" | custom-call | flops 12999999488 | bytes 4000000 | tf_op jit(solution)/shard_map/near_fwd/pallas_call | solution.py:86
  118.2 7.3 %collective-permute-done.10.k_ref.v_ref = bf16[384,1024]{1,0:T(8,128)(2,1)S(1)} collective-permute-done((bf16[384,1024]{1,0:T(8,128)(2,1)S(1)}, bf16[384,1024]{1,0:T(8,128)(2,1)S(1)}, u32[]{:S(2)}, u32[]{:S(2)}) %collective-permute-start.10) | collective-permute-done | bytes 786464 | tf_op jit(solution)/shard_map/ppermute | solution.py:365
  126.3 13.5 %cross_fwd.1 = (bf16[192,2048]{1,0:T(8,128)(2,1)}, f32[3,1,2048]{2,1,0:T(1,128)}) custom-call(s32[7]{0:T(128)} %stack.88.scal, bf16[192,2048]{1,0:T(8,128)(2,1)} %get-tuple-element.210.q_ref, bf16[384,1024]{1,0:T(8,128)(2,1)} %copy-done.95, bf16[384,1024]{1,0:T(8,128)(2,1)} %copy-done.95, f32[192,2048]{1,0:T(8,128)} %get-tuple-element.35.o1_ref, ...), custom_call_target="tpu_custom_call" | custom-call | flops 3300000000 | bytes 4000000 | tf_op jit(solution)/shard_map/cross_fwd/pallas_call | solution.py:158
  139.8 2.7 reshape.624
  147.4 6.7 %collective-permute-done.11 = bf16[192,2,2,256]{3,0,2,1:T(8,128)(2,1)S(1)} collective-permute-done((bf16[192,2,2,256]{3,0,2,1:T(8,128)(2,1)S(1)}, bf16[192,2,2,256]{3,0,2,1:T(8,128)(2,1)S(1)}, u32[]{:S(2)}, u32[]{:S(2)}) %collective-permute-start.11) | collective-permute-done | bytes 393248 | tf_op jit(solution)/shard_map/ppermute | solution.py:365
  157.5 5.2 dynamic-slice_bitcast_fusion.2
  168.6 2.2 fusion.105
  171.6 2.2 fusion.107
  206.1 2.4 fusion.99
  208.7 21.1 %fusion.98 = (f32[512]{0:T(512)S(1)}, f32[512]{0:T(512)S(1)}, f32[512,3072]{1,0:T(8,128)S(1)}, f32[512,3072]{1,0:T(8,128)}, f32[512,3072]{1,0:T(8,128)}) fusion(f32[3072]{0:T(1024)S(1)} %bitcast.306, bf16[768,768]{1,0:T(8,128)(2,1)S(1)} %bitcast.279, bf16[768,768]{1,0:T(8,128)(2,1)S(1)} %bitcast.277, bf16[768,768]{1,0:T(8,128)(2,1)S(1)} %bitcast.275, ...), kind=kOutput, calls=%fused_computation.287 | convolution fusion | flops 2543713280 | bytes 25192448 | tf_op jit(solution)/shard_map/dot_general | solution.py:547
  229.9 8.2 %fusion.6 = (bf16[3072]{0:T(1024)(128)(2,1)S(1)}, f32[512]{0:T(512)S(1)}, f32[512]{0:T(512)S(1)}, bf16[512,3072]{1,0:T(8,128)(2,1)}, f32[3072,512]{0,1:T(8,128)}) fusion(f32[512,3072]{1,0:T(8,128)S(1)} %get-tuple-element.176, f32[512]{0:T(512)S(1)} %get-tuple-element.267, f32[512]{0:T(512)S(1)} %get-tuple-element.266, f32[3072]{0:T(1024)S(1)} %bitcast.304, ...), kind=kOutput, calls=%fused_computation.12 | convolution fusion | flops 2452090880 | bytes 21272576 | tf_op jit(solution)/shard_map/dot_general | solution.py:556
  238.2 3.1 reduce_sum.303
  241.3 10.9 %fusion.100 = (bf16[3072]{0:T(1024)(128)(2,1)S(1)}, bf16[512,3072]{1,0:T(8,128)(2,1)S(1)}) fusion(f32[512,3072]{1,0:T(8,128)} %get-tuple-element.177, f32[512]{0:T(512)S(1)} %broadcast_multiply_fusion.2, f32[512,3072]{1,0:T(8,128)} %copy-done.5, f32[512]{0:T(512)S(1)} %get-tuple-element.266, f32[512]{0:T(512)S(1)} %broadcast_multiply_fusion.3, ...), kind=kLoop, calls=%fused_computation.289 | loop fusion | flops 36172800 | bytes 28350464 | tf_op jit(solution)/shard_map/reduce_sum | solution.py:560
  252.3 3.0 multiply_reduce_fusion.2
  255.3 4.9 convolution_convert_fusion.1
  261.1 4.2 fusion.35
  275.3 4.5 fusion.13
  280.4 4.2 fusion.104
  289.9 4.2 fusion.103
  294.1 4.3 concatenate.132
  298.4 3.7 concatenate.131
  302.1 5.4 concatenate.130
  310.6 14.0 %cross_bwd.1 = (f32[192,1024]{1,0:T(8,128)}, bf16[192,1024]{1,0:T(8,128)(2,1)}, bf16[192,1024]{1,0:T(8,128)(2,1)}) custom-call(s32[7]{0:T(128)} %stack.88.scal, bf16[192,2048]{1,0:T(8,128)(2,1)} %get-tuple-element.210.q_ref, bf16[384,1024]{1,0:T(8,128)(2,1)} %copy-done.95, bf16[384,1024]{1,0:T(8,128)(2,1)} %copy-done.95, bf16[192,2048]{1,0:T(8,128)(2,1)} %reshape.659.do_ref, ...), custom_call_target="tpu_custom_call" | custom-call | flops 8000000000 | bytes 6000000 | tf_op jit(solution)/shard_map/cross_bwd/pallas_call | solution.py:323
  325.9 40.9 %near_bwd.1 = (bf16[192,2048]{1,0:T(8,128)(2,1)}, f32[192,2048]{1,0:T(8,128)}, f32[192,2048]{1,0:T(8,128)}) custom-call(s32[7]{0:T(128)} %stack.88.scal, bf16[192,2048]{1,0:T(8,128)(2,1)} %get-tuple-element.210.q_ref, bf16[192,2048]{1,0:T(8,128)(2,1)} %get-tuple-element.209.k_ref, bf16[192,2048]{1,0:T(8,128)(2,1)} %get-tuple-element.208.v_ref, ...), custom_call_target="tpu_custom_call" | custom-call | flops 32000000000 | bytes 8000000 | tf_op jit(solution)/shard_map/near_bwd/pallas_call | solution.py:249
  368.0 2.5 broadcast_select_fusion
  377.5 6.1 %fusion.119 = (bf16[768,576]{0,1:T(8,128)(2,1)}, f32[768,576]{0,1:T(8,128)}) fusion(bf16[2048,768]{1,0:T(8,128)(2,1)} %slice_dynamic-update-slice_fusion, f32[768]{0:T(1024)} %copy-done.86, f32[768]{0:T(1024)S(1)} %copy-done.65, f32[2048]{0:T(1024)} %copy-done.84, f32[2048]{0:T(1024)} %copy-done.83, bf16[384,2048]{1,0:T(8,128)(2,1)} %copy-done.8, ...), kind=kOutput, calls=%fused_computation.306 | convolution fusion | flops 1826537472 | bytes 8181760 | tf_op jit(solution)/shard_map/dot_general | solution.py:355
  383.6 3.0 copy.184
  386.7 2.4 fusion.16
  396.0 4.4 collective-permute-start.18
  400.5 4.1 collective-permute-start.24
  406.0 2.7 fusion.55
  408.9 2.5 copy-done
  412.8 3.0 collective-permute-start.21
  415.8 4.0 add_convert_fusion.3
  419.8 3.4 collective-permute-start.20
  423.2 3.1 collective-permute-start.19
  426.3 2.5 collective-permute-done.22
  428.8 3.2 collective-permute-done.21
  434.5 3.2 add_convert_fusion.5
  439.7 4.6 concatenate.129
  447.7 2.4 fusion.42
  454.9 55.8 %collective-permute-done.26 = f32[2,96]{1,0:T(2,128)S(1)} collective-permute-done((f32[2,96]{1,0:T(2,128)S(1)}, f32[2,96]{1,0:T(2,128)S(1)}, u32[]{:S(2)}, u32[]{:S(2)}) %collective-permute-start.26) | collective-permute-done | bytes 800 | tf_op jit(solution)/shard_map/ppermute | solution.py:365
  511.3 2.7 multiply_reduce_fusion.5
  514.1 3.7 add_convert_fusion.2
  519.4 3.3 collective-permute-start.36
  524.2 2.9 collective-permute-start.33
  527.2 7.5 %collective-permute-done.30 = bf16[96,1792]{1,0:T(8,128)(2,1)S(1)} collective-permute-done((bf16[96,1792]{1,0:T(8,128)(2,1)S(1)}, bf16[96,1792]{1,0:T(8,128)(2,1)S(1)}, u32[]{:S(2)}, u32[]{:S(2)}) %collective-permute-start.30) | collective-permute-done | bytes 344096 | tf_op jit(solution)/shard_map/ppermute | solution.py:365
  534.7 26.6 %collective-permute-start.31 = (bf16[96,1792]{1,0:T(8,128)(2,1)S(1)}, bf16[96,1792]{1,0:T(8,128)(2,1)}, u32[]{:S(2)}, u32[]{:S(2)}) collective-permute-start(bf16[96,1792]{1,0:T(8,128)(2,1)S(1)} %get-tuple-element.207), channel_id=1, source_target_pairs={{0,8},{4,12},{8,0},{12,4},{16,24},{20,28},{24,16},{28,20},{1,9},{5... | collective-permute-start | bytes 1032200 | tf_op jit(solution)/shard_map/ppermute | solution.py:365
  562.0 2.4 copy.183
  564.4 3.1 reshape.663
  567.5 7.6 %collective-permute-done.34 = bf16[96,1792]{1,0:T(8,128)(2,1)} collective-permute-done((bf16[96,1792]{1,0:T(8,128)(2,1)}, bf16[96,1792]{1,0:T(8,128)(2,1)}, u32[]{:S(2)}, u32[]{:S(2)}) %collective-permute-start.34) | collective-permute-done | bytes 344096 | tf_op jit(solution)/shard_map/ppermute | solution.py:365
  575.1 4.1 collective-permute-done.33
  (470 shorter events, 133.8 us)
Async XLA Ops:
  7.3 150.2 %all-gather.3.cloned.1.call-start = ((), (), s32[]{:S(2)}) async-start(), calls=%async_computation | async-start | bytes 13246464 | tf_op jit(solution)/shard_map/all_gather | solution.py:497
  14.3 45.0 %copy-start.96 = (s32[4]{0:T(128)S(1)}, s32[4]{0:T(128)}, u32[]{:S(2)}) copy-start(s32[4]{0:T(128)} %param.43) | copy-start | bytes 52
  18.3 124.9 %copy-start.1 = (bf16[256,2,768]{2,1,0:T(2,128)(2,1)}, bf16[256,2,768]{2,1,0:T(2,128)(2,1)S(1)}, u32[]{:S(2)}) copy-start(bf16[256,2,768]{2,1,0:T(2,128)(2,1)S(1)} %reshape.620) | copy-start | bytes 2359300
  18.4 187.6 %copy-start.3 = (bf16[256,2,768]{2,0,1:T(8,128)(2,1)}, bf16[256,2,768]{2,0,1:T(8,128)(2,1)S(1)}, u32[]{:S(2)}) copy-start(bf16[256,2,768]{2,0,1:T(8,128)(2,1)S(1)} %copy.249) | copy-start | bytes 2359300
  18.4 54.3 %collective-permute-start.8 = (bf16[512,768]{1,0:T(8,128)(2,1)S(1)}, bf16[512,768]{1,0:T(8,128)(2,1)S(1)}, u32[]{:S(2)}, u32[]{:S(2)}) collective-permute-start(bf16[512,768]{1,0:T(8,128)(2,1)S(1)} %bitcast.230), channel_id=1, source_target_pairs={{0,2},{1,3},{2,0},{3,1},{4,6},{5,7},{6,4},{7,5},{8,10},{9,11},{10,... | collective-permute-start | bytes 2359304 | tf_op jit(solution)/shard_map/ppermute | solution.py:365
  21.7 47.7 %copy-start.43 = (bf16[112,576]{1,0:T(8,128)(2,1)}, bf16[112,576]{1,0:T(8,128)(2,1)S(1)}, u32[]{:S(2)}) copy-start(bf16[112,576]{1,0:T(8,128)(2,1)S(1)} %fusion.68.refs_0_) | copy-start | bytes 387076
  21.7 10.8 %collective-permute-start.6 = (bf16[112,576]{1,0:T(8,128)(2,1)S(1)}, bf16[112,576]{1,0:T(8,128)(2,1)S(1)}, u32[]{:S(2)}, u32[]{:S(2)}) collective-permute-start(bf16[112,576]{1,0:T(8,128)(2,1)S(1)} %fusion.68.refs_0_), channel_id=1, source_target_pairs={{0,28},{4,24},{8,20},{12,16},{16,12},{20,8},{24,4},{28,0},{1,29},{... | collective-permute-start | bytes 387080 | tf_op jit(solution)/shard_map/ppermute | solution.py:365
  26.3 22.7 %collective-permute-start.5 = (bf16[112,576]{1,0:T(8,128)(2,1)S(1)}, bf16[112,576]{1,0:T(8,128)(2,1)S(1)}, u32[]{:S(2)}, u32[]{:S(2)}) collective-permute-start(bf16[112,576]{1,0:T(8,128)(2,1)S(1)} %fusion.68.refs_0_), channel_id=1, source_target_pairs={{0,24},{4,28},{8,16},{12,20},{16,8},{20,12},{24,0},{28,4},{1,25},{... | collective-permute-start | bytes 387080 | tf_op jit(solution)/shard_map/ppermute | solution.py:365
  26.5 30.3 %collective-permute-start.4 = (bf16[112,576]{1,0:T(8,128)(2,1)S(1)}, bf16[112,576]{1,0:T(8,128)(2,1)S(1)}, u32[]{:S(2)}, u32[]{:S(2)}) collective-permute-start(bf16[112,576]{1,0:T(8,128)(2,1)S(1)} %fusion.68.refs_0_), channel_id=1, source_target_pairs={{0,20},{4,16},{8,28},{12,24},{16,4},{20,0},{24,12},{28,8},{1,21},{... | collective-permute-start | bytes 387080 | tf_op jit(solution)/shard_map/ppermute | solution.py:365
  27.3 31.8 %collective-permute-start.3 = (bf16[112,576]{1,0:T(8,128)(2,1)S(1)}, bf16[112,576]{1,0:T(8,128)(2,1)}, u32[]{:S(2)}, u32[]{:S(2)}) collective-permute-start(bf16[112,576]{1,0:T(8,128)(2,1)S(1)} %fusion.68.refs_0_), channel_id=1, source_target_pairs={{0,16},{4,20},{8,24},{12,28},{16,0},{20,4},{24,8},{28,12},{1,17},{... | collective-permute-start | bytes 387080 | tf_op jit(solution)/shard_map/ppermute | solution.py:365
  32.5 36.9 %copy-start.56 = (bf16[112,576]{1,0:T(8,128)(2,1)}, bf16[112,576]{1,0:T(8,128)(2,1)S(1)}, u32[]{:S(2)}) copy-start(bf16[112,576]{1,0:T(8,128)(2,1)S(1)} %collective-permute-done.6.refs_7_) | copy-start | bytes 387076
  32.5 28.7 %collective-permute-start.2 = (bf16[112,576]{1,0:T(8,128)(2,1)S(1)}, bf16[112,576]{1,0:T(8,128)(2,1)}, u32[]{:S(2)}, u32[]{:S(2)}) collective-permute-start(bf16[112,576]{1,0:T(8,128)(2,1)S(1)} %fusion.68.refs_0_), channel_id=1, source_target_pairs={{0,12},{4,8},{8,4},{12,0},{16,28},{20,24},{24,20},{28,16},{1,13},{... | collective-permute-start | bytes 387080 | tf_op jit(solution)/shard_map/ppermute | solution.py:365
  49.0 20.4 %collective-permute-start.1 = (bf16[112,576]{1,0:T(8,128)(2,1)S(1)}, bf16[112,576]{1,0:T(8,128)(2,1)}, u32[]{:S(2)}, u32[]{:S(2)}) collective-permute-start(bf16[112,576]{1,0:T(8,128)(2,1)S(1)} %fusion.68.refs_0_), channel_id=1, source_target_pairs={{0,8},{4,12},{8,0},{12,4},{16,24},{20,28},{24,16},{28,20},{1,9},{5... | collective-permute-start | bytes 387080 | tf_op jit(solution)/shard_map/ppermute | solution.py:365
  56.9 12.5 %collective-permute-start = (bf16[112,576]{1,0:T(8,128)(2,1)S(1)}, bf16[112,576]{1,0:T(8,128)(2,1)}, u32[]{:S(2)}, u32[]{:S(2)}) collective-permute-start(bf16[112,576]{1,0:T(8,128)(2,1)S(1)} %fusion.68.refs_0_), channel_id=1, source_target_pairs={{0,4},{4,0},{8,12},{12,8},{16,20},{20,16},{24,28},{28,24},{1,5},{5... | collective-permute-start | bytes 387080 | tf_op jit(solution)/shard_map/ppermute | solution.py:365
  59.1 14.8 %collective-permute-start.7 = (bf16[512,768]{1,0:T(8,128)(2,1)S(1)}, bf16[512,768]{1,0:T(8,128)(2,1)S(1)}, u32[]{:S(2)}, u32[]{:S(2)}) collective-permute-start(bf16[512,768]{1,0:T(8,128)(2,1)S(1)} %bitcast.232), channel_id=1, source_target_pairs={{0,1},{1,0},{2,3},{3,2},{4,5},{5,4},{6,7},{7,6},{8,9},{9,8},{10,11... | collective-permute-start | bytes 2359304 | tf_op jit(solution)/shard_map/ppermute | solution.py:365
  72.7 2.8 collective-permute-start.9
  88.3 37.2 %collective-permute-start.10 = (bf16[384,1024]{1,0:T(8,128)(2,1)S(1)}, bf16[384,1024]{1,0:T(8,128)(2,1)S(1)}, u32[]{:S(2)}, u32[]{:S(2)}) collective-permute-start(bf16[384,1024]{1,0:T(8,128)(2,1)S(1)} %slice_select_fusion), channel_id=1, source_target_pairs={{0,4},{4,0},{8,12},{12,8},{16,20},{20,16},{24,28},{28,24},{1,5},{5... | collective-permute-start | bytes 2359304 | tf_op jit(solution)/shard_map/ppermute | solution.py:365
  143.2 10.9 %collective-permute-start.11 = (bf16[192,2,2,256]{3,0,2,1:T(8,128)(2,1)S(1)}, bf16[192,2,2,256]{3,0,2,1:T(8,128)(2,1)S(1)}, u32[]{:S(2)}, u32[]{:S(2)}) collective-permute-start(bf16[192,2,2,256]{3,0,2,1:T(8,128)(2,1)S(1)} %copy.207), channel_id=1, source_target_pairs={{0,2},{1,3},{2,0},{3,1},{4,6},{5,7},{6,4},{7,5},{8,10},{9,11},{10,... | collective-permute-start | bytes 1179656 | tf_op jit(solution)/shard_map/ppermute | solution.py:365
  154.2 2.0 collective-permute-start.12
  203.7 61.7 %copy-start.71 = (f32[768]{0:T(1024)}, f32[768]{0:T(1024)S(1)}, u32[]{:S(2)}) copy-start(f32[768]{0:T(1024)S(1)} %get-tuple-element.167) | copy-start | bytes 9220
  208.5 21.3 %copy-start.15 = (f32[512,768]{1,0:T(8,128)}, f32[512,768]{1,0:T(8,128)S(1)}, u32[]{:S(2)}) copy-start(f32[512,768]{1,0:T(8,128)S(1)} %get-tuple-element.272) | copy-start | bytes 4718596
  208.6 21.2 %copy-start.20 = (bf16[8,96,768]{2,1,0:T(8,128)(2,1)S(1)}, bf16[8,96,768]{2,1,0:T(8,128)(2,1)}, u32[]{:S(2)}) copy-start(bf16[8,96,768]{2,1,0:T(8,128)(2,1)} %get-tuple-element.191) | copy-start | bytes 3538948
  208.6 21.2 %copy-start.22 = (bf16[8,96,768]{2,1,0:T(8,128)(2,1)S(1)}, bf16[8,96,768]{2,1,0:T(8,128)(2,1)}, u32[]{:S(2)}) copy-start(bf16[8,96,768]{2,1,0:T(8,128)(2,1)} %get-tuple-element.284) | copy-start | bytes 3538948
  274.8 9.8 %collective-permute-start.13 = (bf16[2,192,2,256]{3,1,2,0:T(8,128)(2,1)}, bf16[2,192,2,256]{3,1,2,0:T(8,128)(2,1)}, u32[]{:S(2)}, u32[]{:S(2)}) collective-permute-start(bf16[2,192,2,256]{3,1,2,0:T(8,128)(2,1)} %pad_maximum_fusion.15), channel_id=1, source_target_pairs={{0,1},{1,0},{2,3},{3,2},{4,5},{5,4},{6,7},{7,6},{8,9},{9,8},{10,11... | collective-permute-start | bytes 1179656 | tf_op jit(solution)/shard_map/ppermute | solution.py:365
  287.2 20.3 %collective-permute-start.14 = (bf16[192,2,2,256]{3,0,2,1:T(8,128)(2,1)}, bf16[192,2,2,256]{3,0,2,1:T(8,128)(2,1)}, u32[]{:S(2)}, u32[]{:S(2)}) collective-permute-start(bf16[192,2,2,256]{3,0,2,1:T(8,128)(2,1)} %pad_maximum_fusion.16), channel_id=1, source_target_pairs={{0,2},{1,3},{2,0},{3,1},{4,6},{5,7},{6,4},{7,5},{8,10},{9,11},{10,... | collective-permute-start | bytes 1179656 | tf_op jit(solution)/shard_map/ppermute | solution.py:365
  298.4 114.4 %collective-permute-start.28 = (bf16[768,1792]{1,0:T(8,128)(2,1)}, bf16[768,1792]{1,0:T(8,128)(2,1)}, u32[]{:S(2)}, u32[]{:S(2)}) collective-permute-start(bf16[768,1792]{1,0:T(8,128)(2,1)} %concatenate.132), channel_id=1, source_target_pairs={{0,1},{1,0},{2,3},{3,2},{4,5},{5,4},{6,7},{7,6},{8,9},{9,8},{10,11... | collective-permute-start | bytes 8257544 | tf_op jit(solution)/shard_map/ppermute | solution.py:365
  325.8 40.9 %collective-permute-start.15 = (bf16[384,1024]{1,0:T(8,128)(2,1)S(1)}, bf16[384,1024]{1,0:T(8,128)(2,1)}, u32[]{:S(2)}, u32[]{:S(2)}) collective-permute-start(bf16[384,1024]{1,0:T(8,128)(2,1)S(1)} %pad_maximum_fusion.11), channel_id=1, source_target_pairs={{0,4},{4,0},{8,12},{12,8},{16,20},{20,16},{24,28},{28,24},{1,5},{5... | collective-permute-start | bytes 2359304 | tf_op jit(solution)/shard_map/ppermute | solution.py:365
  396.0 23.7 %collective-permute-start.18 = (bf16[96,640]{0,1:T(8,128)(2,1)S(1)}, bf16[96,640]{0,1:T(8,128)(2,1)S(1)}, u32[]{:S(2)}, u32[]{:S(2)}) collective-permute-start(bf16[96,640]{0,1:T(8,128)(2,1)S(1)} %get-tuple-element.215), channel_id=1, source_target_pairs={{0,4},{4,0},{8,12},{12,8},{16,20},{20,16},{24,28},{28,24},{1,5},{5... | collective-permute-start | bytes 368648 | tf_op jit(solution)/shard_map/ppermute | solution.py:365
  400.5 19.3 %collective-permute-start.24 = (bf16[96,640]{0,1:T(8,128)(2,1)S(1)}, bf16[96,640]{0,1:T(8,128)(2,1)S(1)}, u32[]{:S(2)}, u32[]{:S(2)}) collective-permute-start(bf16[96,640]{0,1:T(8,128)(2,1)S(1)} %get-tuple-element.216), channel_id=1, source_target_pairs={{0,28},{4,24},{8,20},{12,16},{16,12},{20,8},{24,4},{28,0},{1,29},{... | collective-permute-start | bytes 368648 | tf_op jit(solution)/shard_map/ppermute | solution.py:365
  404.6 18.7 %collective-permute-start.23 = (bf16[96,640]{0,1:T(8,128)(2,1)S(1)}, bf16[96,640]{0,1:T(8,128)(2,1)S(1)}, u32[]{:S(2)}, u32[]{:S(2)}) collective-permute-start(bf16[96,640]{0,1:T(8,128)(2,1)S(1)} %get-tuple-element.217), channel_id=1, source_target_pairs={{0,24},{4,28},{8,16},{12,20},{16,8},{20,12},{24,0},{28,4},{1,25},{... | collective-permute-start | bytes 368648 | tf_op jit(solution)/shard_map/ppermute | solution.py:365
  405.1 23.6 %collective-permute-start.22 = (bf16[96,640]{0,1:T(8,128)(2,1)S(1)}, bf16[96,640]{0,1:T(8,128)(2,1)S(1)}, u32[]{:S(2)}, u32[]{:S(2)}) collective-permute-start(bf16[96,640]{0,1:T(8,128)(2,1)S(1)} %get-tuple-element.218), channel_id=1, source_target_pairs={{0,20},{4,16},{8,28},{12,24},{16,4},{20,0},{24,12},{28,8},{1,21},{... | collective-permute-start | bytes 368648 | tf_op jit(solution)/shard_map/ppermute | solution.py:365
  411.5 23.0 %copy-start.98 = (bf16[512,3072]{1,0:T(8,128)(2,1)S(1)}, bf16[512,3072]{1,0:T(8,128)(2,1)}, u32[]{:S(2)}) copy-start(bf16[512,3072]{1,0:T(8,128)(2,1)} %get-tuple-element.182) | copy-start | bytes 9437188
  412.8 21.6 %copy-start.17 = (f32[512,768]{1,0:T(8,128)S(1)}, f32[512,768]{1,0:T(8,128)}, u32[]{:S(2)}) copy-start(f32[512,768]{1,0:T(8,128)} %copy-done.15) | copy-start | bytes 4718596
  412.8 21.6 %copy-start.21 = (bf16[8,96,768]{2,1,0:T(8,128)(2,1)S(1)}, bf16[8,96,768]{2,1,0:T(8,128)(2,1)}, u32[]{:S(2)}) copy-start(bf16[8,96,768]{2,1,0:T(8,128)(2,1)} %get-tuple-element.191) | copy-start | bytes 3538948
  412.8 21.6 %copy-start.23 = (bf16[8,96,768]{2,1,0:T(8,128)(2,1)S(1)}, bf16[8,96,768]{2,1,0:T(8,128)(2,1)}, u32[]{:S(2)}) copy-start(bf16[8,96,768]{2,1,0:T(8,128)(2,1)} %get-tuple-element.284) | copy-start | bytes 3538948
  412.8 21.6 %copy-start.25 = (bf16[8,96,768]{2,1,0:T(8,128)(2,1)S(1)}, bf16[8,96,768]{2,1,0:T(8,128)(2,1)}, u32[]{:S(2)}) copy-start(bf16[8,96,768]{2,1,0:T(8,128)(2,1)} %get-tuple-element.195) | copy-start | bytes 3538948
  412.8 21.6 %copy-start.27 = (bf16[8,96,768]{2,1,0:T(8,128)(2,1)S(1)}, bf16[8,96,768]{2,1,0:T(8,128)(2,1)}, u32[]{:S(2)}) copy-start(bf16[8,96,768]{2,1,0:T(8,128)(2,1)} %get-tuple-element.286) | copy-start | bytes 3538948
  412.8 21.6 %copy-start.87 = (f32[768]{0:T(1024)S(1)}, f32[768]{0:T(1024)}, u32[]{:S(2)}) copy-start(f32[768]{0:T(1024)} %add.389) | copy-start | bytes 9220
  412.8 19.2 %collective-permute-start.21 = (bf16[96,640]{0,1:T(8,128)(2,1)S(1)}, bf16[96,640]{0,1:T(8,128)(2,1)S(1)}, u32[]{:S(2)}, u32[]{:S(2)}) collective-permute-start(bf16[96,640]{0,1:T(8,128)(2,1)S(1)} %get-tuple-element.219), channel_id=1, source_target_pairs={{0,16},{4,20},{8,24},{12,28},{16,0},{20,4},{24,8},{28,12},{1,17},{... | collective-permute-start | bytes 368648 | tf_op jit(solution)/shard_map/ppermute | solution.py:365
  419.8 94.3 %collective-permute-start.27 = (bf16[768,1792]{1,0:T(8,128)(2,1)}, bf16[768,1792]{1,0:T(8,128)(2,1)}, u32[]{:S(2)}, u32[]{:S(2)}) collective-permute-start(bf16[768,1792]{1,0:T(8,128)(2,1)} %concatenate.130), channel_id=1, source_target_pairs={{0,1},{1,0},{2,3},{3,2},{4,5},{5,4},{6,7},{7,6},{8,9},{9,8},{10,11... | collective-permute-start | bytes 8257544 | tf_op jit(solution)/shard_map/ppermute | solution.py:365
  419.8 24.5 %collective-permute-start.20 = (bf16[96,640]{0,1:T(8,128)(2,1)}, bf16[96,640]{0,1:T(8,128)(2,1)}, u32[]{:S(2)}, u32[]{:S(2)}) collective-permute-start(bf16[96,640]{0,1:T(8,128)(2,1)} %get-tuple-element.220), channel_id=1, source_target_pairs={{0,12},{4,8},{8,4},{12,0},{16,28},{20,24},{24,20},{28,16},{1,13},{... | collective-permute-start | bytes 368648 | tf_op jit(solution)/shard_map/ppermute | solution.py:365
  423.2 21.1 %collective-permute-start.19 = (bf16[96,640]{0,1:T(8,128)(2,1)}, bf16[96,640]{0,1:T(8,128)(2,1)}, u32[]{:S(2)}, u32[]{:S(2)}) collective-permute-start(bf16[96,640]{0,1:T(8,128)(2,1)} %get-tuple-element.221), channel_id=1, source_target_pairs={{0,8},{4,12},{8,0},{12,4},{16,24},{20,28},{24,16},{28,20},{1,9},{5... | collective-permute-start | bytes 368648 | tf_op jit(solution)/shard_map/ppermute | solution.py:365
  428.8 17.2 %collective-permute-start.16 = (bf16[2,2,256,768]{3,2,1,0:T(8,128)(2,1)}, bf16[2,2,256,768]{3,2,1,0:T(8,128)(2,1)}, u32[]{:S(2)}, u32[]{:S(2)}) collective-permute-start(bf16[2,2,256,768]{3,2,1,0:T(8,128)(2,1)} %pad_maximum_fusion.3), channel_id=1, source_target_pairs={{0,1},{1,0},{2,3},{3,2},{4,5},{5,4},{6,7},{7,6},{8,9},{9,8},{10,11... | collective-permute-start | bytes 4718600 | tf_op jit(solution)/shard_map/ppermute | solution.py:365
  432.7 81.4 %collective-permute-start.29 = (bf16[768,1792]{1,0:T(8,128)(2,1)}, bf16[768,1792]{1,0:T(8,128)(2,1)}, u32[]{:S(2)}, u32[]{:S(2)}) collective-permute-start(bf16[768,1792]{1,0:T(8,128)(2,1)} %add_convert_fusion.3), channel_id=1, source_target_pairs={{0,2},{1,3},{2,0},{3,1},{4,6},{5,7},{6,4},{7,5},{8,10},{9,11},{10,... | collective-permute-start | bytes 8257544 | tf_op jit(solution)/shard_map/ppermute | solution.py:365
  445.8 4.6 collective-permute-start.25
  447.6 63.1 %copy-start.90 = (bf16[96]{0:T(256)(128)(2,1)S(1)}, bf16[96]{0:T(256)(128)(2,1)}, u32[]{:S(2)}) copy-start(bf16[96]{0:T(256)(128)(2,1)} %param.24) | copy-start | bytes 580
  447.7 63.1 %copy-start.92 = (bf16[96]{0:T(256)(128)(2,1)S(1)}, bf16[96]{0:T(256)(128)(2,1)}, u32[]{:S(2)}) copy-start(bf16[96]{0:T(256)(128)(2,1)} %param.23) | copy-start | bytes 580
  447.7 63.7 %copy-start.79 = (f32[2,256]{1,0:T(2,128)S(1)}, f32[2,256]{1,0:T(2,128)}, u32[]{:S(2)}) copy-start(f32[2,256]{1,0:T(2,128)} %get-tuple-element.263) | copy-start | bytes 6148
  447.7 63.7 %copy-start.80 = (f32[2,256]{1,0:T(2,128)S(1)}, f32[2,256]{1,0:T(2,128)}, u32[]{:S(2)}) copy-start(f32[2,256]{1,0:T(2,128)} %get-tuple-element.265) | copy-start | bytes 6148
  450.1 61.2 %collective-permute-start.17 = (bf16[2,256,768]{2,1,0:T(8,128)(2,1)}, bf16[2,256,768]{2,1,0:T(8,128)(2,1)}, u32[]{:S(2)}, u32[]{:S(2)}) collective-permute-start(bf16[2,256,768]{2,1,0:T(8,128)(2,1)} %fusion.42), channel_id=1, source_target_pairs={{0,2},{1,3},{2,0},{3,1},{4,6},{5,7},{6,4},{7,5},{8,10},{9,11},{10,... | collective-permute-start | bytes 2359304 | tf_op jit(solution)/shard_map/ppermute | solution.py:365
  450.4 60.3 %collective-permute-start.26 = (f32[2,96]{1,0:T(2,128)S(1)}, f32[2,96]{1,0:T(2,128)S(1)}, u32[]{:S(2)}, u32[]{:S(2)}) collective-permute-start(f32[2,96]{1,0:T(2,128)S(1)} %fusion.92), channel_id=1, source_target_pairs={{0,2},{1,3},{2,0},{3,1},{4,6},{5,7},{6,4},{7,5},{8,10},{9,11},{10,... | collective-permute-start | bytes 2312 | tf_op jit(solution)/shard_map/ppermute | solution.py:365
  517.8 43.5 %copy-start.4 = (bf16[256,2,768]{2,0,1:T(8,128)(2,1)S(1)}, bf16[256,2,768]{2,0,1:T(8,128)(2,1)}, u32[]{:S(2)}) copy-start(bf16[256,2,768]{2,0,1:T(8,128)(2,1)} %copy-done.3) | copy-start | bytes 2359300
  517.8 43.5 %copy-start.7 = (f32[512,768]{1,0:T(8,128)S(1)}, f32[512,768]{1,0:T(8,128)}, u32[]{:S(2)}) copy-start(f32[512,768]{1,0:T(8,128)} %copy-done.6) | copy-start | bytes 4718596
  517.8 43.5 %copy-start.70 = (f32[1,2,2,128]{3,1,2,0:T(2,128)S(1)}, f32[1,2,2,128]{3,1,2,0:T(2,128)}, u32[]{:S(2)}) copy-start(f32[1,2,2,128]{3,1,2,0:T(2,128)} %copy-done.69) | copy-start | bytes 6148
  517.8 43.5 %copy-start.78 = (f32[512]{0:T(512)S(1)}, f32[512]{0:T(512)}, u32[]{:S(2)}) copy-start(f32[512]{0:T(512)} %add_rsqrt_fusion.2) | copy-start | bytes 6148
  518.9 15.8 %collective-permute-start.30 = (bf16[96,1792]{1,0:T(8,128)(2,1)S(1)}, bf16[96,1792]{1,0:T(8,128)(2,1)S(1)}, u32[]{:S(2)}, u32[]{:S(2)}) collective-permute-start(bf16[96,1792]{1,0:T(8,128)(2,1)S(1)} %get-tuple-element.201), channel_id=1, source_target_pairs={{0,4},{4,0},{8,12},{12,8},{16,20},{20,16},{24,28},{28,24},{1,5},{5... | collective-permute-start | bytes 1032200 | tf_op jit(solution)/shard_map/ppermute | solution.py:365
  519.4 15.3 %collective-permute-start.36 = (bf16[96,1792]{1,0:T(8,128)(2,1)S(1)}, bf16[96,1792]{1,0:T(8,128)(2,1)S(1)}, u32[]{:S(2)}, u32[]{:S(2)}) collective-permute-start(bf16[96,1792]{1,0:T(8,128)(2,1)S(1)} %get-tuple-element.202), channel_id=1, source_target_pairs={{0,28},{4,24},{8,20},{12,16},{16,12},{20,8},{24,4},{28,0},{1,29},{... | collective-permute-start | bytes 1032200 | tf_op jit(solution)/shard_map/ppermute | solution.py:365
  522.8 44.7 %collective-permute-start.35 = (bf16[96,1792]{1,0:T(8,128)(2,1)}, bf16[96,1792]{1,0:T(8,128)(2,1)}, u32[]{:S(2)}, u32[]{:S(2)}) collective-permute-start(bf16[96,1792]{1,0:T(8,128)(2,1)} %get-tuple-element.203), channel_id=1, source_target_pairs={{0,24},{4,28},{8,16},{12,20},{16,8},{20,12},{24,0},{28,4},{1,25},{... | collective-permute-start | bytes 1032200 | tf_op jit(solution)/shard_map/ppermute | solution.py:365
  524.2 50.9 %collective-permute-start.34 = (bf16[96,1792]{1,0:T(8,128)(2,1)}, bf16[96,1792]{1,0:T(8,128)(2,1)}, u32[]{:S(2)}, u32[]{:S(2)}) collective-permute-start(bf16[96,1792]{1,0:T(8,128)(2,1)} %get-tuple-element.204), channel_id=1, source_target_pairs={{0,20},{4,16},{8,28},{12,24},{16,4},{20,0},{24,12},{28,8},{1,21},{... | collective-permute-start | bytes 1032200 | tf_op jit(solution)/shard_map/ppermute | solution.py:365
  524.2 55.0 %collective-permute-start.33 = (bf16[96,1792]{1,0:T(8,128)(2,1)}, bf16[96,1792]{1,0:T(8,128)(2,1)}, u32[]{:S(2)}, u32[]{:S(2)}) collective-permute-start(bf16[96,1792]{1,0:T(8,128)(2,1)} %get-tuple-element.205), channel_id=1, source_target_pairs={{0,16},{4,20},{8,24},{12,28},{16,0},{20,4},{24,8},{28,12},{1,17},{... | collective-permute-start | bytes 1032200 | tf_op jit(solution)/shard_map/ppermute | solution.py:365
  534.7 26.6 %copy-start.44 = (bf16[96,1792]{1,0:T(8,128)(2,1)}, bf16[96,1792]{1,0:T(8,128)(2,1)S(1)}, u32[]{:S(2)}) copy-start(bf16[96,1792]{1,0:T(8,128)(2,1)S(1)} %collective-permute-done.30) | copy-start | bytes 1032196
  534.7 44.5 %collective-permute-start.32 = (bf16[96,1792]{1,0:T(8,128)(2,1)S(1)}, bf16[96,1792]{1,0:T(8,128)(2,1)}, u32[]{:S(2)}, u32[]{:S(2)}) collective-permute-start(bf16[96,1792]{1,0:T(8,128)(2,1)S(1)} %get-tuple-element.206), channel_id=1, source_target_pairs={{0,12},{4,8},{8,4},{12,0},{16,28},{20,24},{24,20},{28,16},{1,13},{... | collective-permute-start | bytes 1032200 | tf_op jit(solution)/shard_map/ppermute | solution.py:365
  534.7 26.6 %copy-start.45 = (bf16[96,1792]{1,0:T(8,128)(2,1)}, bf16[96,1792]{1,0:T(8,128)(2,1)S(1)}, u32[]{:S(2)}) copy-start(bf16[96,1792]{1,0:T(8,128)(2,1)S(1)} %collective-permute-done.36) | copy-start | bytes 1032196
  534.7 46.0 %collective-permute-start.31 = (bf16[96,1792]{1,0:T(8,128)(2,1)S(1)}, bf16[96,1792]{1,0:T(8,128)(2,1)}, u32[]{:S(2)}, u32[]{:S(2)}) collective-permute-start(bf16[96,1792]{1,0:T(8,128)(2,1)S(1)} %get-tuple-element.207), channel_id=1, source_target_pairs={{0,8},{4,12},{8,0},{12,4},{16,24},{20,28},{24,16},{28,20},{1,9},{5... | collective-permute-start | bytes 1032200 | tf_op jit(solution)/shard_map/ppermute | solution.py:365
  (73 other events, 489.7 us)
Sparse Core Ops, SparseCore 0:
  16.3 124.7 all-gather.2
